TPU v7x, 256 devices: a whole 4x4x8 slice. The times are simulated.
256 devices in a mesh: expert: 32 (over y, z_lo, x), replica: 8 (over z_hi, core).
Axes of the slice: x: 4, y: 4, z: 8 (z_hi: 4, z_lo: 2; z = z_hi * 2 + z_lo), core: 2. Of those that a mesh axis runs over, the one named last changes fastest.
Arguments:
- tokens: bfloat16 [4096, 4096], P('expert', 'replica'), may hold values from -6 to 6
- out_grad: bfloat16 [4096, 4096], P('expert', 'replica'), may hold values from -6 to 6
- expert_ids: int32 [4096, 8], P('expert'), may hold values from 0 to 63, all different within a row; in each aligned block of 128 rows (0 to 127, 128 to 255, ...) at most 20 rows name the same one
- route_weight: float32 [4096, 8], P('expert'), may hold values from 0.05 to 0.3
- gate_weight: bfloat16 [64, 4096, 768], P('expert', 'replica'), may hold values from -0.09375 to 0.09375
- up_weight: bfloat16 [64, 4096, 768], P('expert', 'replica'), may hold values from -0.09375 to 0.09375
- down_weight: bfloat16 [64, 768, 4096], P('expert', None, 'replica'), may hold values from -0.21875 to 0.21875
Outputs:
- mixed: bfloat16 [4096, 4096], P('expert', 'replica')
- in_grad: bfloat16 [4096, 4096], P('expert', 'replica')
- grad_gate: bfloat16 [64, 4096, 768], P('expert', 'replica')
- grad_up: bfloat16 [64, 4096, 768], P('expert', 'replica')
- grad_down: bfloat16 [64, 768, 4096], P('expert', None, 'replica')
Inputs may be any that keep to these rules, and one draw needn't show every extreme that they name: `expert_ids`: each token names 8 different experts. Within the 128 rows of one index of expert no expert is named more than 20 times, a bound that some block reaches.
All inputs are finite; a program needn't handle non-finite values.
Results may differ from a plain program's by a relative error of at most 0.0064.
Values may be sent and summed in bfloat16 or wider, within the bound.
No kernel may reach another device: no remote copies, remote signals or barrier semaphores. Data moves between devices by JAX's collectives and lax.ppermute only.
A program may use at most 128 MiB of HBM per device.

v0:
```python
import functools
import jax
import jax.numpy as jnp
from jax import lax
from jax.experimental import pallas as pl
from jax.experimental.pallas import tpu as pltpu
from jax.sharding import Mesh, PartitionSpec as P


F32 = jnp.float32
BF16 = jnp.bfloat16
CORES = 2


def dot(a, b, ca, cb):
    return lax.dot_general(a, b, (((ca,), (cb,)), ((), ())), preferred_element_type=F32)


def split3(w):
    hi = w.astype(BF16)
    rest = w - hi.astype(F32)
    mid = rest.astype(BF16)
    low = (rest - mid.astype(F32)).astype(BF16)
    return hi, mid, low


def chunk_rows(where, away, chips, rows):
    return pl.ds(pl.multiple_of((where[0] + away) % chips * rows, 16), rows)


class Rows:
    def __init__(self, blocks, experts, cap):
        self.blocks, self.experts = blocks, experts
        self.main = cap // 8 * 8
        self.rest = cap - self.main
        self.tile = experts * self.rest
        self.per = blocks * self.main
        self.tail = blocks * self.tile
        self.start = experts * self.per
        self.half = self.start + self.tail

    def tail_of(self, e):
        row = lax.broadcasted_iota(jnp.int32, (self.tail, 1), 0)
        return row % self.tile // self.rest == e

    def of_expert(self, ref, e):
        return jnp.concatenate([ref[e * self.per:(e + 1) * self.per, :], ref[self.start:, :]], axis=0)

    def tails(self, totals):
        out = totals[0][self.per:]
        for e in range(1, self.experts):
            out = jnp.where(self.tail_of(e), totals[e][self.per:], out)
        return out

    def regroup(self, read, out):
        for j in range(self.blocks):
            for e in range(self.experts):
                out[e * self.per + j * self.main:e * self.per + (j + 1) * self.main, :] = (
                    read(j)[e * self.main:(e + 1) * self.main, :])
        first = self.experts * self.main
        for j in range(0, self.blocks, 2):
            pair = jnp.concatenate([read(j)[first:, :], read(j + 1)[first:, :]], axis=0)
            out[self.start + j * self.tile:self.start + (j + 2) * self.tile, :] = pair

    def ungroup(self, totals, out):
        tails = self.tails(totals)
        first = self.experts * self.main
        for j in range(self.blocks):
            for e in range(self.experts):
                out[j, e * self.main:(e + 1) * self.main, :] = totals[e][j * self.main:(j + 1) * self.main]
            out[j, first:, :] = tails[j * self.tile:(j + 1) * self.tile]


def regroup_kernel(lay, where, x_ref, keep_ref, give_ref):
    for out, core in ((keep_ref, where[1]), (give_ref, 1 - where[1])):
        lay.regroup(lambda j: x_ref[core * lay.blocks + j], out)


def regroup(where, x, lay):
    vmem = pl.BlockSpec(memory_space=pltpu.VMEM)
    shape = jax.ShapeDtypeStruct((lay.half, x.shape[2]), BF16)
    return pl.pallas_call(
        functools.partial(regroup_kernel, lay),
        in_specs=[pl.BlockSpec(memory_space=pltpu.SMEM), vmem],
        out_specs=[vmem, vmem],
        out_shape=[shape, shape],
        name="regroup",
    )(where, x)


def gate_up_kernel(lay, where, x_ref, other_ref, gm, go, um, uo, up_ref, down_ref, keep_ref, own_ref, x_by, acc):
    rows = own_ref.shape[1]
    chips = lay.half // rows

    @pl.when(pl.program_id(0) == 0)
    def _():
        for e in range(lay.experts):
            x_by[e] = lay.of_expert(x_ref, e)
            x_by[lay.experts + e] = lay.of_expert(other_ref, e)

    for i, (wm, wo) in enumerate(((gm, go), (um, uo))):
        totals = []
        for e in range(lay.experts):
            total = dot(x_by[e], wm[e], 1, 0) + dot(x_by[lay.experts + e], wo[e], 1, 0)
            acc[i, e * lay.per:(e + 1) * lay.per, :] = total[:lay.per]
            totals.append(total)
        acc[i, lay.start:, :] = lay.tails(totals)
    at = functools.partial(chunk_rows, where, chips=chips, rows=rows)
    up_ref[0] = acc[0, at(2), :].astype(BF16)
    up_ref[1] = acc[1, at(1), :].astype(BF16)
    down_ref[0] = acc[1, at(2), :].astype(BF16)
    down_ref[1] = acc[0, at(chips - 1), :].astype(BF16)
    keep_ref[0] = acc[0, at(1), :]
    keep_ref[1] = acc[1, at(chips - 1), :]
    own_ref[0] = acc[0, at(0), :]
    own_ref[1] = acc[1, at(0), :]


def gate_up(where, x, other, gm, go, um, uo, lay, rows):
    experts, feats, width = gm.shape
    tile = 256
    weight = pl.BlockSpec((experts, feats, tile), lambda n, w: (0, 0, n))
    out = pl.BlockSpec((2, rows, tile), lambda n, w: (0, 0, n))
    shape = (2, rows, width)
    return pl.pallas_call(
        functools.partial(gate_up_kernel, lay),
        grid_spec=pltpu.PrefetchScalarGridSpec(
            num_scalar_prefetch=1,
            grid=(width // tile,),
            in_specs=[
                pl.BlockSpec(x.shape, lambda n, w: (0, 0)),
                pl.BlockSpec(other.shape, lambda n, w: (0, 0)),
                weight, weight, weight, weight,
            ],
            out_specs=[out, out, out, out],
            scratch_shapes=[
                pltpu.VMEM((2 * experts, lay.per + lay.tail, feats), BF16),
                pltpu.VMEM((2, lay.half, tile), F32),
            ],
        ),
        out_shape=[
            jax.ShapeDtypeStruct(shape, BF16),
            jax.ShapeDtypeStruct(shape, BF16),
            jax.ShapeDtypeStruct(shape, F32),
            jax.ShapeDtypeStruct(shape, F32),
        ],
        name="gate_up",
    )(where, x, other, gm, go, um, uo)


def hidden_grad_kernel(lay, where, g_ref, other_ref, dm, do, up_ref, down_ref, keep_ref, own_ref, g_by, acc):
    part = own_ref.shape[1]
    rows = 2 * part
    chips = lay.half // rows

    @pl.when(pl.program_id(0) == 0)
    def _():
        for e in range(lay.experts):
            g_by[e] = lay.of_expert(g_ref, e)
            g_by[lay.experts + e] = lay.of_expert(other_ref, e)

    totals = []
    for e in range(lay.experts):
        total = dot(g_by[e], dm[e], 1, 1) + dot(g_by[lay.experts + e], do[e], 1, 1)
        acc[e * lay.per:(e + 1) * lay.per, :] = total[:lay.per]
        totals.append(total)
    acc[lay.start:, :] = lay.tails(totals)

    def at(away, k):
        start = (where[0] + away) % chips * rows + k * part
        return acc[pl.ds(pl.multiple_of(start, 16), part), :]

    up_ref[0] = at(2, 0).astype(BF16)
    up_ref[1] = at(1, 1).astype(BF16)
    down_ref[0] = at(2, 1).astype(BF16)
    down_ref[1] = at(chips - 1, 0).astype(BF16)
    keep_ref[0] = at(1, 0)
    keep_ref[1] = at(chips - 1, 1)
    own_ref[0] = at(0, 0)
    own_ref[1] = at(0, 1)


def hidden_grad_parts(where, g, other, dm, do, lay, rows):
    experts, width, feats = dm.shape
    tile = 256
    weight = pl.BlockSpec((experts, tile, feats), lambda n, w: (0, n, 0))
    out = pl.BlockSpec((2, rows // 2, tile), lambda n, w: (0, 0, n))
    shape = (2, rows // 2, width)
    return pl.pallas_call(
        functools.partial(hidden_grad_kernel, lay),
        grid_spec=pltpu.PrefetchScalarGridSpec(
            num_scalar_prefetch=1,
            grid=(width // tile,),
            in_specs=[
                pl.BlockSpec(g.shape, lambda n, w: (0, 0)),
                pl.BlockSpec(other.shape, lambda n, w: (0, 0)),
                weight, weight,
            ],
            out_specs=[out, out, out, out],
            scratch_shapes=[
                pltpu.VMEM((2 * experts, lay.per + lay.tail, feats), BF16),
                pltpu.VMEM((lay.half, tile), F32),
            ],
        ),
        out_shape=[
            jax.ShapeDtypeStruct(shape, BF16),
            jax.ShapeDtypeStruct(shape, BF16),
            jax.ShapeDtypeStruct(shape, F32),
            jax.ShapeDtypeStruct(shape, F32),
        ],
        name="hidden_grad",
    )(where, g, other, dm, do)


def gather_rows(where, put_to, own, low, high, far, chips, rows):
    def put(away, value, skip=0):
        start = (where[0] + away) % chips * rows + skip
        put_to(pl.ds(pl.multiple_of(start, 16), value.shape[0]), value)

    put(0, own)
    put(chips - 1, low)
    put(1, high)
    skip = 0
    for value in far:
        put(2, value, skip)
        skip += value.shape[0]


def expert_out_kernel(lay, where, own, low, high, far_a, far_b, dm, do, mine_ref, other_ref, all_ref):
    rows = own.shape[0]

    def put_to(at, value):
        all_ref[at, :] = value

    gather_rows(where, put_to, own[...], low[...], high[...], (far_a[...], far_b[...]), lay.half // rows, rows)
    for out, weight in ((mine_ref, dm), (other_ref, do)):
        totals = [dot(lay.of_expert(all_ref, e), weight[e], 1, 0).astype(BF16) for e in range(lay.experts)]
        lay.ungroup(totals, out)


def expert_out_of(where, pieces, dm, do, lay):
    experts, width, feats = dm.shape
    vmem = pl.BlockSpec(memory_space=pltpu.VMEM)
    out = jax.ShapeDtypeStruct((lay.blocks, experts * lay.main + lay.tile, feats), BF16)
    return pl.pallas_call(
        functools.partial(expert_out_kernel, lay),
        in_specs=[pl.BlockSpec(memory_space=pltpu.SMEM)] + [vmem] * 7,
        out_specs=[vmem] * 3,
        out_shape=[out, out, jax.ShapeDtypeStruct((lay.half, width), BF16)],
        name="expert_out",
    )(where, *pieces, dm, do)


def slot_in_kernel(lay, where, own, low, high, far_g, far_u, gm, go, um, uo, mine_ref, other_ref, all_ref):
    rows = own.shape[1]
    for i, far in enumerate((far_g, far_u)):

        def put_to(at, value):
            all_ref[i, at, :] = value

        gather_rows(where, put_to, own[i], low[i], high[i], (far[...],), lay.half // rows, rows)
    for out, gw, uw in ((mine_ref, gm, um), (other_ref, go, uo)):
        totals = []
        for e in range(lay.experts):
            total = dot(lay.of_expert(all_ref.at[0], e), gw[e], 1, 1)
            totals.append((total + dot(lay.of_expert(all_ref.at[1], e), uw[e], 1, 1)).astype(BF16))
        lay.ungroup(totals, out)


def slot_in_of(where, pieces, gm, go, um, uo, lay):
    experts, feats, width = gm.shape
    vmem = pl.BlockSpec(memory_space=pltpu.VMEM)
    out = jax.ShapeDtypeStruct((lay.blocks, experts * lay.main + lay.tile, feats), BF16)
    return pl.pallas_call(
        functools.partial(slot_in_kernel, lay),
        in_specs=[pl.BlockSpec(memory_space=pltpu.SMEM)] + [vmem] * 9,
        out_specs=[vmem] * 3,
        out_shape=[out, out, jax.ShapeDtypeStruct((2, lay.half, width), BF16)],
        name="slot_in",
    )(where, *pieces, gm, go, um, uo)


def weight_grad_kernel(lay, a_own, a_far, b_own, b_far, out_ref, a_by, b_by):
    e = pl.program_id(0)
    main = pl.ds(pl.multiple_of(e * lay.per, 16), lay.per)
    at = [pl.ds(0, lay.per), pl.ds(lay.per, lay.per)]
    rest = [pl.ds(2 * lay.per, lay.tail), pl.ds(2 * lay.per + lay.tail, lay.tail)]

    @pl.when(pl.program_id(1) == 0)
    def _():
        for k, ref in enumerate((a_own, a_far)):
            a_by[at[k], :] = ref[main, :]
            tail = ref[lay.start:, :]
            a_by[rest[k], :] = jnp.where(lay.tail_of(e), tail, jnp.zeros_like(tail))

    for k, ref in enumerate((b_own, b_far)):
        b_by[at[k], :] = ref[0, main, :]
        b_by[rest[k], :] = ref[0, lay.start:, :]
    out_ref[0] = dot(a_by[...], b_by[...], 0, 0).astype(BF16)


def weight_grad(a_own, a_far, b_own, b_far, i, lay):
    rows = 2 * (lay.per + lay.tail)
    a_cols, b_cols = a_own.shape[1], b_own.shape[2]
    tile = 256
    a_spec = pl.BlockSpec(a_own.shape, lambda e, n: (0, 0))
    b_spec = pl.BlockSpec((1, lay.half, tile), lambda e, n: (i, 0, n))
    return pl.pallas_call(
        functools.partial(weight_grad_kernel, lay),
        grid=(lay.experts, b_cols // tile),
        in_specs=[a_spec, a_spec, b_spec, b_spec],
        out_specs=pl.BlockSpec((1, a_cols, tile), lambda e, n: (e, 0, n)),
        out_shape=jax.ShapeDtypeStruct((lay.experts, a_cols, b_cols), BF16),
        scratch_shapes=[pltpu.VMEM((rows, a_cols), BF16), pltpu.VMEM((rows, tile), BF16)],
        name="weight_grad",
    )(a_own, a_far, b_own, b_far)


def routing(ids, weight, owner, rank, allowed, block, experts_all):
    rows = ids.shape[0]
    experts = jnp.arange(experts_all, dtype=jnp.int32)
    hit = ids[:, :, None] == experts[None, None, :]
    member = jnp.any(hit, axis=1)
    t_row = lax.broadcasted_iota(jnp.int32, (rows, rows), 0)
    t_col = lax.broadcasted_iota(jnp.int32, (rows, rows), 1)
    earlier = ((t_col <= t_row) & (t_col // block == t_row // block)).astype(BF16)
    rank1 = jnp.where(member, dot(earlier, member.astype(BF16), 1, 0), 0.0)
    spread = (experts[:, None] == owner[None, :]).astype(BF16)
    rank1_s = dot(rank1.astype(BF16), spread, 1, 0)
    taken = rank1_s == (rank + 1).astype(F32)[None, :]
    if allowed is not None:
        taken = taken & allowed
    if weight is None:
        return taken.astype(BF16)
    weight_te = jnp.sum(jnp.where(hit, weight[:, :, None], 0.0), axis=1)
    weight_s = sum(dot(part, spread, 1, 0) for part in split3(weight_te))
    return taken.astype(BF16), jnp.where(taken, weight_s, 0.0)


def weighted_sum(weight_s, rows):
    return sum(dot(part, rows, 1, 0) for part in split3(weight_s))


def layer(tokens, out_grad, expert_ids, route_weight, gate_weight, up_weight, down_weight):
    n_y, n_z, n_x = (lax.axis_size(a) for a in ("y", "z_lo", "x"))
    n_cols = n_y * n_z * n_x
    n_reps = lax.axis_size("replica")
    tok_count, topk = expert_ids.shape
    local_experts, feats, _ = gate_weight.shape
    experts_all = local_experts * n_cols
    cap = tok_count * topk * 5 // (4 * experts_all)
    slots = experts_all * cap
    rows = slots // n_reps

    rep = lax.axis_index("replica")
    core = rep % CORES
    where = jnp.stack([rep // CORES, core]).astype(jnp.int32)
    to_swap = [(r, r ^ 1) for r in range(n_reps)]
    to_up = [(r, (r + CORES) % n_reps) for r in range(n_reps)]
    to_down = [(r, (r - CORES) % n_reps) for r in range(n_reps)]

    def swap(a):
        return lax.ppermute(a, "replica", to_swap)

    def up_one(a):
        return lax.ppermute(a, "replica", to_up)

    def down_one(a):
        return lax.ppermute(a, "replica", to_down)

    def tree_sum(send_up, send_down, keep, own):
        low = up_one(send_up)
        high = down_one(send_down)
        first = up_one((keep[0] + low[0].astype(F32)).astype(BF16))
        second = down_one((keep[1] + high[0].astype(F32)).astype(BF16))
        a = own[0] + high[1].astype(F32) + first.astype(F32)
        b = own[1] + low[1].astype(F32) + second.astype(F32)
        return a, b

    plane = n_y * n_x
    z_lo = lax.axis_index("z_lo")
    to_plane = [(z, n_z - 1 - z) for z in range(n_z)]
    lay = Rows(n_cols // CORES, local_experts, cap)

    def cross(a):
        return lax.ppermute(a, "z_lo", to_plane)

    def by_plane(mine, far):
        first = lax.select_n(z_lo == 0, far, mine)
        return jnp.concatenate([first, lax.select_n(z_lo == 0, mine, far)], axis=0)

    gate_other = swap(gate_weight)
    up_other = swap(up_weight)
    down_other = swap(down_weight)
    pairs = jnp.concatenate([expert_ids.astype(F32), route_weight], axis=1)
    pairs_other = cross(pairs)
    out_grad_other = cross(out_grad)

    block_rows = local_experts * cap
    slot = jnp.arange(slots, dtype=jnp.int32)
    at, inner = slot // block_rows, slot % block_rows
    first = local_experts * lay.main
    which = jnp.where(inner < first, inner // lay.main, (inner - first) // lay.rest)
    rank = jnp.where(inner < first, inner % lay.main, lay.main + (inner - first) % lay.rest)

    def owner_of(z):
        return (((at // n_z // n_x) * n_z + z) * n_x + at // n_z % n_x) * local_experts + which

    picker = routing(expert_ids, None, owner_of(at % n_z), rank, None, tok_count, experts_all)
    send_x = dot(picker, tokens, 0, 0).astype(BF16)

    def exchange(a):
        a = a.reshape(n_cols, block_rows, feats)
        return lax.all_to_all(a, ("y", "x", "z_lo"), split_axis=0, concat_axis=0, tiled=True)

    def exchange_plane(a):
        a = a.reshape(plane, n_z * block_rows, feats)
        return lax.all_to_all(a, ("y", "x"), split_axis=0, concat_axis=0, tiled=True)

    def both_halves(mine, other):
        got = swap(other)
        return jnp.concatenate(
            [lax.select_n(core == 0, got, mine), lax.select_n(core == 0, mine, got)], axis=0)

    recv_x = exchange(send_x)
    x_keep, x_give = regroup(where, recv_x, lay)
    x_other = swap(x_give)

    token = jnp.arange(n_z * tok_count, dtype=jnp.int32)
    same = token[:, None] // tok_count == at[None, :] % n_z
    pairs2 = by_plane(pairs, pairs_other)
    picker2, weight2 = routing(
        pairs2[:, :topk].astype(jnp.int32), pairs2[:, topk:],
        owner_of(z_lo), rank, same, tok_count, experts_all)
    picked_g = dot(picker2, by_plane(out_grad, out_grad_other), 0, 0)
    send_g = (jnp.sum(weight2, axis=0)[:, None] * picked_g).astype(BF16)
    recv_g = exchange_plane(send_g).reshape(n_cols, block_rows, feats)

    gate, up = tree_sum(*gate_up(
        where, x_keep, x_other, gate_weight, gate_other, up_weight, up_other, lay, rows))

    g_keep, g_give = regroup(where, recv_g, lay)
    g_other = swap(g_give)
    grad_a, grad_b = tree_sum(*hidden_grad_parts(where, g_keep, g_other, down_weight, down_other, lay, rows))
    hidden_grad = jnp.concatenate([grad_a, grad_b], axis=0)

    own = (gate * jax.nn.sigmoid(gate) * up).astype(BF16)
    low, high = up_one(own), down_one(own)
    far_a, far_b = up_one(low[:rows // 2]), down_one(high[rows // 2:])
    mine, other, hidden = expert_out_of(
        where, (own, low, high, far_a, far_b), down_weight, down_other, lay)
    expert_out = both_halves(mine, other)
    returned = exchange_plane(expert_out).reshape(slots, feats)
    sums = weighted_sum(weight2, returned).reshape(n_z, tok_count, feats)
    sum_mine = lax.select_n(z_lo == 0, sums[1], sums[0])
    from_far = cross(lax.select_n(z_lo == 0, sums[0], sums[1]))

    gate, up = lax.optimization_barrier((gate, up))
    sig = jax.nn.sigmoid(gate)
    gate_grad = (hidden_grad * up * sig * (1.0 + gate * (1.0 - sig))).astype(BF16)
    up_grad = (hidden_grad * (gate * sig)).astype(BF16)
    own = jnp.stack([gate_grad, up_grad])
    low, high = up_one(own), down_one(own)
    far_g, far_u = up_one(low[0]), down_one(high[1])
    mine, other, grads = slot_in_of(
        where, (own, low, high, far_g, far_u), gate_weight, gate_other, up_weight, up_other, lay)
    slot_in = both_halves(mine, other)
    back_in = exchange(slot_in).reshape(slots, feats)
    in_grad = dot(picker, back_in, 1, 0).astype(BF16)

    hidden_other = swap(hidden)
    grad_down = weight_grad(hidden, hidden_other, g_keep[None], g_give[None], 0, lay)
    grads_other = swap(grads)
    grad_gate = weight_grad(x_keep, x_give, grads, grads_other, 0, lay)
    grad_up = weight_grad(x_keep, x_give, grads, grads_other, 1, lay)
    grad_up, sum_mine = lax.optimization_barrier((grad_up, sum_mine))
    mixed = (sum_mine + from_far).astype(BF16)
    return (mixed, in_grad, grad_gate, grad_up, grad_down)


def solution(mesh):
    n_y, n_z, n_x = 4, 2, 4
    devices = mesh.devices.reshape(n_y, n_z, n_x, mesh.shape["replica"])
    mesh = Mesh(devices, ("y", "z_lo", "x", "replica"))
    cols = ("y", "z_lo", "x")
    in_specs = (
        P(cols, "replica"),
        P(cols, "replica"),
        P(cols, None),
        P(cols, None),
        P(cols, "replica", None),
        P(cols, "replica", None),
        P(cols, None, "replica"),
    )
    out_specs = (
        P(cols, "replica"),
        P(cols, "replica"),
        P(cols, "replica", None),
        P(cols, "replica", None),
        P(cols, None, "replica"),
    )
    return jax.shard_map(layer, mesh=mesh, in_specs=in_specs, out_specs=out_specs, check_vma=False)
```

profile of v0, /device:TPU:1, one launch (start us, length us, event | category | flops | bytes accessed | tf_op | source)
XLA Modules:
  0.0 245.8 jit_solution(16745116926802903621)
XLA Ops:
  3.6 9.3 %all-to-all-start = ((bf16[32,40,512]{2,1,0:T(8,128)(2,1)}), bf16[32,40,512]{2,1,0:T(8,128)(2,1)S(1)}, u32[]{:S(2)}, u32[]{:S(2)}) async-start(bf16[32,40,512]{2,1,0:T(8,128)(2,1)} %bitcast.2), calls=%async_computation | async-start | bytes 2621440 | tf_op jit(solution)/shard_map/all_to_all | solution.py:414
  14.6 13.8 %collective-permute-done = f32[128,16]{0,1:T(8,128)S(1)} collective-permute-done((f32[128,16]{0,1:T(8,128)S(1)}, f32[128,16]{0,1:T(8,128)S(1)}, u32[]{:S(2)}, u32[]{:S(2)}) %collective-permute-start) | collective-permute-done | bytes 8224 | tf_op jit(solution)/shard_map/ppermute | solution.py:386
  34.9 6.7 %all-to-all-start.1 = ((bf16[16,80,512]{2,1,0:T(8,128)(2,1)}), bf16[16,80,512]{2,1,0:T(8,128)(2,1)}, u32[]{:S(2)}, u32[]{:S(2)}) async-start(bf16[16,80,512]{2,1,0:T(8,128)(2,1)} %bitcast.51), calls=%async_computation.1 | async-start | bytes 2621440 | tf_op jit(solution)/shard_map/all_to_all | solution.py:418
  48.1 10.8 %all-to-all-done.1 = bf16[16,80,512]{2,1,0:T(8,128)(2,1)} async-done(((bf16[16,80,512]{2,1,0:T(8,128)(2,1)}), bf16[16,80,512]{2,1,0:T(8,128)(2,1)}, u32[]{:S(2)}, u32[]{:S(2)}) %all-to-all-start.1) | async-done | bytes 1310752 | tf_op jit(solution)/shard_map/all_to_all | solution.py:418
  61.4 4.3 %collective-permute-start.2 = (bf16[640,512]{1,0:T(8,128)(2,1)}, bf16[640,512]{1,0:T(8,128)(2,1)}, u32[]{:S(2)}, u32[]{:S(2)}) collective-permute-start(bf16[640,512]{1,0:T(8,128)(2,1)} %get-tuple-element.30), channel_id=1, source_target_pairs={{0,1},{1,0},{2,3},{3,2},{4,5},{5,4},{6,7},{7,6},{8,9},{9,8},{10,11... | collective-permute-start | bytes 1966088 | tf_op jit(solution)/shard_map/ppermute | solution.py:363
  65.7 7.8 %gate_up.1 = (bf16[2,160,768]{2,1,0:T(8,128)(2,1)}, bf16[2,160,768]{2,1,0:T(8,128)(2,1)}, f32[2,160,768]{2,1,0:T(8,128)}, f32[2,160,768]{2,1,0:T(8,128)}) custom-call(s32[2]{0:T(128)} %pad_add_fusion.where, bf16[640,512]{1,0:T(8,128)(2,1)} %get-tuple-element.27.x_ref.a_own, bf16[640,512]{1,0:T(8,128)(2,1)} %collective-permute-done.8.other_ref, ...), custom_call_target="tpu_custom_call" | custom-call | tf_op jit(solution)/shard_map/gate_up/pallas_call | solution.py:125
  73.5 5.1 %collective-permute-start.11 = (bf16[2,160,768]{2,1,0:T(8,128)(2,1)}, bf16[2,160,768]{2,1,0:T(8,128)(2,1)}, u32[]{:S(2)}, u32[]{:S(2)}) collective-permute-start(bf16[2,160,768]{2,1,0:T(8,128)(2,1)} %get-tuple-element.36), channel_id=1, source_target_pairs={{0,6},{1,7},{2,0},{3,1},{4,2},{5,3},{6,4},{7,5},{8,14},{9,15},{10,... | collective-permute-start | bytes 1474568 | tf_op jit(solution)/shard_map/ppermute | solution.py:369
  78.6 5.8 %hidden_grad.1 = (bf16[2,80,768]{2,1,0:T(8,128)(2,1)}, bf16[2,80,768]{2,1,0:T(8,128)(2,1)}, f32[2,80,768]{2,1,0:T(8,128)}, f32[2,80,768]{2,1,0:T(8,128)}) custom-call(s32[2]{0:T(128)} %pad_add_fusion.where, bf16[640,512]{1,0:T(8,128)(2,1)} %get-tuple-element.29.g_ref, bf16[640,512]{1,0:T(8,128)(2,1)} %collective-permute-done.2.other_ref, ...), custom_call_target="tpu_custom_call" | custom-call | tf_op jit(solution)/shard_map/hidden_grad/pallas_call | solution.py:189
  84.5 3.6 %collective-permute-start.4 = (bf16[2,80,768]{2,1,0:T(8,128)(2,1)}, bf16[2,80,768]{2,1,0:T(8,128)(2,1)S(1)}, u32[]{:S(2)}, u32[]{:S(2)}) collective-permute-start(bf16[2,80,768]{2,1,0:T(8,128)(2,1)} %get-tuple-element.32), channel_id=1, source_target_pairs={{0,6},{1,7},{2,0},{3,1},{4,2},{5,3},{6,4},{7,5},{8,14},{9,15},{10,... | collective-permute-start | bytes 737288 | tf_op jit(solution)/shard_map/ppermute | solution.py:369
  88.1 21.4 %collective-permute-done.4 = bf16[2,80,768]{2,1,0:T(8,128)(2,1)S(1)} collective-permute-done((bf16[2,80,768]{2,1,0:T(8,128)(2,1)}, bf16[2,80,768]{2,1,0:T(8,128)(2,1)S(1)}, u32[]{:S(2)}, u32[]{:S(2)}) %collective-permute-start.4) | collective-permute-done | bytes 245792 | tf_op jit(solution)/shard_map/ppermute | solution.py:369
  109.5 4.6 %collective-permute-done.5 = bf16[2,80,768]{2,1,0:T(8,128)(2,1)S(1)} collective-permute-done((bf16[2,80,768]{2,1,0:T(8,128)(2,1)}, bf16[2,80,768]{2,1,0:T(8,128)(2,1)S(1)}, u32[]{:S(2)}, u32[]{:S(2)}) %collective-permute-start.5) | collective-permute-done | bytes 245792 | tf_op jit(solution)/shard_map/ppermute | solution.py:366
  115.4 3.6 %collective-permute-start.7 = (bf16[80,768]{1,0:T(8,128)(2,1)S(1)}, bf16[80,768]{1,0:T(8,128)(2,1)S(1)}, u32[]{:S(2)}, u32[]{:S(2)}) collective-permute-start(bf16[80,768]{1,0:T(8,128)(2,1)S(1)} %get-tuple-element.65), channel_id=1, source_target_pairs={{0,6},{1,7},{2,0},{3,1},{4,2},{5,3},{6,4},{7,5},{8,14},{9,15},{10,... | collective-permute-start | bytes 368648 | tf_op jit(solution)/shard_map/ppermute | solution.py:369
  120.3 3.6 %collective-permute-start.14 = (bf16[160,768]{1,0:T(8,128)(2,1)S(1)}, bf16[160,768]{1,0:T(8,128)(2,1)S(1)}, u32[]{:S(2)}, u32[]{:S(2)}) collective-permute-start(bf16[160,768]{1,0:T(8,128)(2,1)S(1)} %get-tuple-element.59), channel_id=1, source_target_pairs={{0,6},{1,7},{2,0},{3,1},{4,2},{5,3},{6,4},{7,5},{8,14},{9,15},{10,... | collective-permute-start | bytes 737288 | tf_op jit(solution)/shard_map/ppermute | solution.py:369
  125.2 8.5 %collective-permute-done.13 = bf16[160,768]{1,0:T(8,128)(2,1)S(1)} collective-permute-done((bf16[160,768]{1,0:T(8,128)(2,1)S(1)}, bf16[160,768]{1,0:T(8,128)(2,1)S(1)}, u32[]{:S(2)}, u32[]{:S(2)}) %collective-permute-start.13) | collective-permute-done | bytes 245792 | tf_op jit(solution)/shard_map/ppermute | solution.py:366
  140.5 13.8 %collective-permute-done.20.low = bf16[160,768]{1,0:T(8,128)(2,1)S(1)} collective-permute-done((bf16[160,768]{1,0:T(8,128)(2,1)S(1)}, bf16[160,768]{1,0:T(8,128)(2,1)S(1)}, u32[]{:S(2)}, u32[]{:S(2)}) %collective-permute-start.20) | collective-permute-done | bytes 245792 | tf_op jit(solution)/shard_map/ppermute | solution.py:366
  160.2 13.4 %collective-permute-done.22.far_a = bf16[80,768]{1,0:T(8,128)(2,1)S(1)} collective-permute-done((bf16[80,768]{1,0:T(8,128)(2,1)S(1)}, bf16[80,768]{1,0:T(8,128)(2,1)S(1)}, u32[]{:S(2)}, u32[]{:S(2)}) %collective-permute-start.22) | collective-permute-done | bytes 122912 | tf_op jit(solution)/shard_map/ppermute | solution.py:366
  174.9 4.9 %expert_out.1 = (bf16[16,40,512]{2,1,0:T(8,128)(2,1)}, bf16[16,40,512]{2,1,0:T(8,128)(2,1)}, bf16[640,768]{1,0:T(8,128)(2,1)}) custom-call(s32[2]{0:T(128)} %pad_add_fusion.where, bf16[160,768]{1,0:T(8,128)(2,1)} %copy-done.8, bf16[160,768]{1,0:T(8,128)(2,1)} %copy-done.10, bf16[160,768]{1,0:T(8,128)(2,1)} %copy-done.11, bf16[80,768]{1,0:T(8,128)(2,1)} %copy-done.15, ...), custom_call_target="tpu_custom_call" | custom-call | tf_op jit(solution)/shard_map/expert_out/pallas_call | solution.py:245
  187.6 3.9 %all-to-all-start.2 = ((bf16[16,80,512]{2,1,0:T(8,128)(2,1)}), bf16[16,80,512]{2,1,0:T(8,128)(2,1)S(1)}, u32[]{:S(2)}, u32[]{:S(2)}) async-start(bf16[16,80,512]{2,1,0:T(8,128)(2,1)} %bitcast.49), calls=%async_computation.2 | async-start | bytes 2621440 | tf_op jit(solution)/shard_map/all_to_all | solution.py:418
  191.6 6.3 %collective-permute-done.18.far_u = bf16[160,768]{1,0:T(8,128)(2,1)S(1)} collective-permute-done((bf16[160,768]{1,0:T(8,128)(2,1)S(1)}, bf16[160,768]{1,0:T(8,128)(2,1)S(1)}, u32[]{:S(2)}, u32[]{:S(2)}) %collective-permute-start.18) | collective-permute-done | bytes 245792 | tf_op jit(solution)/shard_map/ppermute | solution.py:369
  198.6 7.8 %slot_in.1 = (bf16[16,40,512]{2,1,0:T(8,128)(2,1)}, bf16[16,40,512]{2,1,0:T(8,128)(2,1)}, bf16[2,640,768]{2,1,0:T(8,128)(2,1)}) custom-call(s32[2]{0:T(128)} %pad_add_fusion.where, bf16[2,160,768]{2,1,0:T(8,128)(2,1)} %copy-done.3, bf16[2,160,768]{2,1,0:T(8,128)(2,1)} %copy-done.4, bf16[2,160,768]{2,1,0:T(8,128)(2,1)} %copy-done.5, ...), custom_call_target="tpu_custom_call" | custom-call | tf_op jit(solution)/shard_map/slot_in/pallas_call | solution.py:274
  211.9 4.7 %all-to-all-start.3 = ((bf16[32,40,512]{2,1,0:T(8,128)(2,1)}), bf16[32,40,512]{2,1,0:T(8,128)(2,1)}, u32[]{:S(2)}, u32[]{:S(2)}) async-start(bf16[32,40,512]{2,1,0:T(8,128)(2,1)} %pad_maximum_fusion.1), calls=%async_computation.3 | async-start | bytes 2621440 | tf_op jit(solution)/shard_map/all_to_all | solution.py:414
  224.0 5.5 %weight_grad.5 = bf16[2,768,512]{2,1,0:T(8,128)(2,1)} custom-call(bf16[640,768]{1,0:T(8,128)(2,1)} %get-tuple-element.48.a_own, bf16[640,768]{1,0:T(8,128)(2,1)} %collective-permute-done.27.a_far, bf16[1,640,512]{2,1,0:T(8,128)(2,1)} %bitcast.50, bf16[1,640,512]{2,1,0:T(8,128)(2,1)} %bitcast.52), custom_call_target="tpu_custom_call" | custom-call | tf_op jit(solution)/shard_map/weight_grad/pallas_call | solution.py:308
  229.4 6.7 %weight_grad.3 = bf16[2,512,768]{2,1,0:T(8,128)(2,1)} custom-call(bf16[640,512]{1,0:T(8,128)(2,1)} %get-tuple-element.27.x_ref.a_own, bf16[640,512]{1,0:T(8,128)(2,1)} %get-tuple-element.28.a_far, bf16[2,640,768]{2,1,0:T(8,128)(2,1)} %get-tuple-element.41.b_own, bf16[2,640,768]{2,1,0:T(8,128)(2,1)} %collective-permute-done.19.b_far), custom_call_target="tpu_custom_call" | custom-call | tf_op jit(solution)/shard_map/weight_grad/pallas_call | solution.py:308
  236.1 6.7 %weight_grad.4 = bf16[2,512,768]{2,1,0:T(8,128)(2,1)} custom-call(bf16[640,512]{1,0:T(8,128)(2,1)} %get-tuple-element.27.x_ref.a_own, bf16[640,512]{1,0:T(8,128)(2,1)} %get-tuple-element.28.a_far, bf16[2,640,768]{2,1,0:T(8,128)(2,1)} %get-tuple-element.41.b_own, bf16[2,640,768]{2,1,0:T(8,128)(2,1)} %collective-permute-done.19.b_far), custom_call_target="tpu_custom_call" | custom-call | tf_op jit(solution)/shard_map/weight_grad/pallas_call | solution.py:308
  (131 shorter events, 62.1 us)
Async XLA Ops:
  3.6 30.2 %all-to-all-start = ((bf16[32,40,512]{2,1,0:T(8,128)(2,1)}), bf16[32,40,512]{2,1,0:T(8,128)(2,1)S(1)}, u32[]{:S(2)}, u32[]{:S(2)}) async-start(bf16[32,40,512]{2,1,0:T(8,128)(2,1)} %bitcast.2), calls=%async_computation | async-start | bytes 2621440 | tf_op jit(solution)/shard_map/all_to_all | solution.py:414
  13.0 15.4 %collective-permute-start = (f32[128,16]{0,1:T(8,128)S(1)}, f32[128,16]{0,1:T(8,128)S(1)}, u32[]{:S(2)}, u32[]{:S(2)}) collective-permute-start(f32[128,16]{0,1:T(8,128)S(1)} %pad_maximum_fusion.5), channel_id=1, source_target_pairs={{0,32},{32,0},{1,33},{33,1},{2,34},{34,2},{3,35},{35,3},{4,36},{36... | collective-permute-start | bytes 24584 | tf_op jit(solution)/shard_map/ppermute | solution.py:386
  14.3 16.9 %collective-permute-start.1 = (bf16[128,512]{1,0:T(8,128)(2,1)S(1)}, bf16[128,512]{1,0:T(8,128)(2,1)}, u32[]{:S(2)}, u32[]{:S(2)}) collective-permute-start(bf16[128,512]{1,0:T(8,128)(2,1)S(1)} %copy-done.14), channel_id=1, source_target_pairs={{0,32},{32,0},{1,33},{33,1},{2,34},{34,2},{3,35},{35,3},{4,36},{36... | collective-permute-start | bytes 393224 | tf_op jit(solution)/shard_map/ppermute | solution.py:386
  34.9 24.0 %all-to-all-start.1 = ((bf16[16,80,512]{2,1,0:T(8,128)(2,1)}), bf16[16,80,512]{2,1,0:T(8,128)(2,1)}, u32[]{:S(2)}, u32[]{:S(2)}) async-start(bf16[16,80,512]{2,1,0:T(8,128)(2,1)} %bitcast.51), calls=%async_computation.1 | async-start | bytes 2621440 | tf_op jit(solution)/shard_map/all_to_all | solution.py:418
  41.6 24.1 %collective-permute-start.10 = (bf16[2,512,768]{2,1,0:T(8,128)(2,1)}, bf16[2,512,768]{2,1,0:T(8,128)(2,1)}, u32[]{:S(2)}, u32[]{:S(2)}) collective-permute-start(bf16[2,512,768]{2,1,0:T(8,128)(2,1)} %um.3), channel_id=1, source_target_pairs={{0,1},{1,0},{2,3},{3,2},{4,5},{5,4},{6,7},{7,6},{8,9},{9,8},{10,11... | collective-permute-start | bytes 4718600 | tf_op jit(solution)/shard_map/ppermute | solution.py:363
  44.4 21.4 %collective-permute-start.9 = (bf16[2,512,768]{2,1,0:T(8,128)(2,1)}, bf16[2,512,768]{2,1,0:T(8,128)(2,1)}, u32[]{:S(2)}, u32[]{:S(2)}) collective-permute-start(bf16[2,512,768]{2,1,0:T(8,128)(2,1)} %gm.3), channel_id=1, source_target_pairs={{0,1},{1,0},{2,3},{3,2},{4,5},{5,4},{6,7},{7,6},{8,9},{9,8},{10,11... | collective-permute-start | bytes 4718600 | tf_op jit(solution)/shard_map/ppermute | solution.py:363
  44.5 34.2 %collective-permute-start.3 = (bf16[2,768,512]{2,1,0:T(8,128)(2,1)S(1)}, bf16[2,768,512]{2,1,0:T(8,128)(2,1)}, u32[]{:S(2)}, u32[]{:S(2)}) collective-permute-start(bf16[2,768,512]{2,1,0:T(8,128)(2,1)S(1)} %copy-done.1), channel_id=1, source_target_pairs={{0,1},{1,0},{2,3},{3,2},{4,5},{5,4},{6,7},{7,6},{8,9},{9,8},{10,11... | collective-permute-start | bytes 4718600 | tf_op jit(solution)/shard_map/ppermute | solution.py:363
  48.0 17.8 %collective-permute-start.8 = (bf16[640,512]{1,0:T(8,128)(2,1)}, bf16[640,512]{1,0:T(8,128)(2,1)}, u32[]{:S(2)}, u32[]{:S(2)}) collective-permute-start(bf16[640,512]{1,0:T(8,128)(2,1)} %get-tuple-element.28.a_far), channel_id=1, source_target_pairs={{0,1},{1,0},{2,3},{3,2},{4,5},{5,4},{6,7},{7,6},{8,9},{9,8},{10,11... | collective-permute-start | bytes 1966088 | tf_op jit(solution)/shard_map/ppermute | solution.py:363
  61.4 17.3 %collective-permute-start.2 = (bf16[640,512]{1,0:T(8,128)(2,1)}, bf16[640,512]{1,0:T(8,128)(2,1)}, u32[]{:S(2)}, u32[]{:S(2)}) collective-permute-start(bf16[640,512]{1,0:T(8,128)(2,1)} %get-tuple-element.30), channel_id=1, source_target_pairs={{0,1},{1,0},{2,3},{3,2},{4,5},{5,4},{6,7},{7,6},{8,9},{9,8},{10,11... | collective-permute-start | bytes 1966088 | tf_op jit(solution)/shard_map/ppermute | solution.py:363
  73.5 45.5 %collective-permute-start.11 = (bf16[2,160,768]{2,1,0:T(8,128)(2,1)}, bf16[2,160,768]{2,1,0:T(8,128)(2,1)}, u32[]{:S(2)}, u32[]{:S(2)}) collective-permute-start(bf16[2,160,768]{2,1,0:T(8,128)(2,1)} %get-tuple-element.36), channel_id=1, source_target_pairs={{0,6},{1,7},{2,0},{3,1},{4,2},{5,3},{6,4},{7,5},{8,14},{9,15},{10,... | collective-permute-start | bytes 1474568 | tf_op jit(solution)/shard_map/ppermute | solution.py:369
  78.6 40.3 %collective-permute-start.12 = (bf16[2,160,768]{2,1,0:T(8,128)(2,1)}, bf16[2,160,768]{2,1,0:T(8,128)(2,1)}, u32[]{:S(2)}, u32[]{:S(2)}) collective-permute-start(bf16[2,160,768]{2,1,0:T(8,128)(2,1)} %get-tuple-element.38), channel_id=1, source_target_pairs={{0,2},{1,3},{2,4},{3,5},{4,6},{5,7},{6,0},{7,1},{8,10},{9,11},{10,... | collective-permute-start | bytes 1474568 | tf_op jit(solution)/shard_map/ppermute | solution.py:366
  84.5 25.1 %collective-permute-start.4 = (bf16[2,80,768]{2,1,0:T(8,128)(2,1)}, bf16[2,80,768]{2,1,0:T(8,128)(2,1)S(1)}, u32[]{:S(2)}, u32[]{:S(2)}) collective-permute-start(bf16[2,80,768]{2,1,0:T(8,128)(2,1)} %get-tuple-element.32), channel_id=1, source_target_pairs={{0,6},{1,7},{2,0},{3,1},{4,2},{5,3},{6,4},{7,5},{8,14},{9,15},{10,... | collective-permute-start | bytes 737288 | tf_op jit(solution)/shard_map/ppermute | solution.py:369
  88.1 26.0 %collective-permute-start.5 = (bf16[2,80,768]{2,1,0:T(8,128)(2,1)}, bf16[2,80,768]{2,1,0:T(8,128)(2,1)S(1)}, u32[]{:S(2)}, u32[]{:S(2)}) collective-permute-start(bf16[2,80,768]{2,1,0:T(8,128)(2,1)} %get-tuple-element.34), channel_id=1, source_target_pairs={{0,2},{1,3},{2,4},{3,5},{4,6},{5,7},{6,0},{7,1},{8,10},{9,11},{10,... | collective-permute-start | bytes 737288 | tf_op jit(solution)/shard_map/ppermute | solution.py:366
  120.2 13.5 %collective-permute-start.13 = (bf16[160,768]{1,0:T(8,128)(2,1)S(1)}, bf16[160,768]{1,0:T(8,128)(2,1)S(1)}, u32[]{:S(2)}, u32[]{:S(2)}) collective-permute-start(bf16[160,768]{1,0:T(8,128)(2,1)S(1)} %get-tuple-element.58), channel_id=1, source_target_pairs={{0,2},{1,3},{2,4},{3,5},{4,6},{5,7},{6,0},{7,1},{8,10},{9,11},{10,... | collective-permute-start | bytes 737288 | tf_op jit(solution)/shard_map/ppermute | solution.py:366
  135.1 19.2 %collective-permute-start.20 = (bf16[160,768]{1,0:T(8,128)(2,1)S(1)}, bf16[160,768]{1,0:T(8,128)(2,1)S(1)}, u32[]{:S(2)}, u32[]{:S(2)}) collective-permute-start(bf16[160,768]{1,0:T(8,128)(2,1)S(1)} %get-tuple-element.49.own), channel_id=1, source_target_pairs={{0,2},{1,3},{2,4},{3,5},{4,6},{5,7},{6,0},{7,1},{8,10},{9,11},{10,... | collective-permute-start | bytes 737288 | tf_op jit(solution)/shard_map/ppermute | solution.py:366
  137.7 16.7 %collective-permute-start.21 = (bf16[160,768]{1,0:T(8,128)(2,1)S(1)}, bf16[160,768]{1,0:T(8,128)(2,1)S(1)}, u32[]{:S(2)}, u32[]{:S(2)}) collective-permute-start(bf16[160,768]{1,0:T(8,128)(2,1)S(1)} %get-tuple-element.49.own), channel_id=1, source_target_pairs={{0,6},{1,7},{2,0},{3,1},{4,2},{5,3},{6,4},{7,5},{8,14},{9,15},{10,... | collective-permute-start | bytes 737288 | tf_op jit(solution)/shard_map/ppermute | solution.py:369
  139.1 41.7 %collective-permute-start.15 = (bf16[2,160,768]{2,1,0:T(8,128)(2,1)S(1)}, bf16[2,160,768]{2,1,0:T(8,128)(2,1)S(1)}, u32[]{:S(2)}, u32[]{:S(2)}) collective-permute-start(bf16[2,160,768]{2,1,0:T(8,128)(2,1)S(1)} %pad_maximum_fusion.3.own), channel_id=1, source_target_pairs={{0,2},{1,3},{2,4},{3,5},{4,6},{5,7},{6,0},{7,1},{8,10},{9,11},{10,... | collective-permute-start | bytes 1474568 | tf_op jit(solution)/shard_map/ppermute | solution.py:366
  154.3 19.3 %collective-permute-start.22 = (bf16[80,768]{1,0:T(8,128)(2,1)S(1)}, bf16[80,768]{1,0:T(8,128)(2,1)S(1)}, u32[]{:S(2)}, u32[]{:S(2)}) collective-permute-start(bf16[80,768]{1,0:T(8,128)(2,1)S(1)} %slice.112), channel_id=1, source_target_pairs={{0,2},{1,3},{2,4},{3,5},{4,6},{5,7},{6,0},{7,1},{8,10},{9,11},{10,... | collective-permute-start | bytes 368648 | tf_op jit(solution)/shard_map/ppermute | solution.py:366
  155.0 18.5 %collective-permute-start.23 = (bf16[80,768]{1,0:T(8,128)(2,1)S(1)}, bf16[80,768]{1,0:T(8,128)(2,1)S(1)}, u32[]{:S(2)}, u32[]{:S(2)}) collective-permute-start(bf16[80,768]{1,0:T(8,128)(2,1)S(1)} %slice.113), channel_id=1, source_target_pairs={{0,6},{1,7},{2,0},{3,1},{4,2},{5,3},{6,4},{7,5},{8,14},{9,15},{10,... | collective-permute-start | bytes 368648 | tf_op jit(solution)/shard_map/ppermute | solution.py:369
  158.1 24.9 %collective-permute-start.16 = (bf16[2,160,768]{2,1,0:T(8,128)(2,1)S(1)}, bf16[2,160,768]{2,1,0:T(8,128)(2,1)S(1)}, u32[]{:S(2)}, u32[]{:S(2)}) collective-permute-start(bf16[2,160,768]{2,1,0:T(8,128)(2,1)S(1)} %pad_maximum_fusion.3.own), channel_id=1, source_target_pairs={{0,6},{1,7},{2,0},{3,1},{4,2},{5,3},{6,4},{7,5},{8,14},{9,15},{10,... | collective-permute-start | bytes 1474568 | tf_op jit(solution)/shard_map/ppermute | solution.py:369
  183.0 14.9 %collective-permute-start.18 = (bf16[160,768]{1,0:T(8,128)(2,1)S(1)}, bf16[160,768]{1,0:T(8,128)(2,1)S(1)}, u32[]{:S(2)}, u32[]{:S(2)}) collective-permute-start(bf16[160,768]{1,0:T(8,128)(2,1)S(1)} %slice_bitcast_fusion), channel_id=1, source_target_pairs={{0,6},{1,7},{2,0},{3,1},{4,2},{5,3},{6,4},{7,5},{8,14},{9,15},{10,... | collective-permute-start | bytes 737288 | tf_op jit(solution)/shard_map/ppermute | solution.py:369
  187.6 24.3 %all-to-all-start.2 = ((bf16[16,80,512]{2,1,0:T(8,128)(2,1)}), bf16[16,80,512]{2,1,0:T(8,128)(2,1)S(1)}, u32[]{:S(2)}, u32[]{:S(2)}) async-start(bf16[16,80,512]{2,1,0:T(8,128)(2,1)} %bitcast.49), calls=%async_computation.2 | async-start | bytes 2621440 | tf_op jit(solution)/shard_map/all_to_all | solution.py:418
  211.9 31.5 %all-to-all-start.3 = ((bf16[32,40,512]{2,1,0:T(8,128)(2,1)}), bf16[32,40,512]{2,1,0:T(8,128)(2,1)}, u32[]{:S(2)}, u32[]{:S(2)}) async-start(bf16[32,40,512]{2,1,0:T(8,128)(2,1)} %pad_maximum_fusion.1), calls=%async_computation.3 | async-start | bytes 2621440 | tf_op jit(solution)/shard_map/all_to_all | solution.py:414
  220.3 22.5 %collective-permute-start.25 = (f32[128,512]{1,0:T(8,128)S(1)}, f32[128,512]{1,0:T(8,128)S(1)}, u32[]{:S(2)}, u32[]{:S(2)}) collective-permute-start(f32[128,512]{1,0:T(8,128)S(1)} %get-tuple-element.60), channel_id=1, source_target_pairs={{0,32},{32,0},{1,33},{33,1},{2,34},{34,2},{3,35},{35,3},{4,36},{36... | collective-permute-start | bytes 786440 | tf_op jit(solution)/shard_map/ppermute | solution.py:386
  (27 other events, 234.2 us)
where the time goes:
time: 247 us; the launch traced here: 246 us
  waiting for transfers between devices  99.7 us (40%)
  starting transfers between devices  69 us (28%)
  Pallas kernels  50 us (20%)
  other arithmetic  12.2 us (5%)
  matrix products  9.5 us (4%)
  local copies, waits for them, and re-layouts  4.43 us (2%)
    ppermute x8, waiting for transfers between devices, up_one(): return lax.ppermute(a, 'replica', to_up)  40.4 us
    ppermute x8, waiting for transfers between devices, down_one(): return lax.ppermute(a, 'replica', to_down)  29 us
    ppermute x8, starting transfers between devices, down_one(): return lax.ppermute(a, 'replica', to_down)  24.3 us
    pallas_call x3, Pallas kernels, weight_grad(): pl.pallas_call(functools.partial(weight_grad_kernel, lay), grid=(lay.expe...  18.8 us
    ppermute x3, waiting for transfers between devices, cross(): return lax.ppermute(a, 'z_lo', to_plane)  14.6 us
    all_to_all x2, starting transfers between devices, exchange(): lax.all_to_all(a, ('y', 'x', 'z_lo'), split_axis=0, concat_axis=0, tiled=...  14 us
    all_to_all x2, waiting for transfers between devices, exchange_plane(): lax.all_to_all(a, ('y', 'x'), split_axis=0, concat_axis=0, tiled=True)  11.5 us
    ppermute x9, starting transfers between devices, swap(): return lax.ppermute(a, 'replica', to_swap)  11.4 us
  transfers between devices with their start and end apart: 32, of which 13 were waited for; matrix products, arithmetic and copies ran while one was open for 6% of the time, Pallas kernels for 20%

commit v1 on v0

--- a/solution.py
+++ b/solution.py
@@ -62,13 +62,13 @@
             pair = jnp.concatenate([read(j)[first:, :], read(j + 1)[first:, :]], axis=0)
             out[self.start + j * self.tile:self.start + (j + 2) * self.tile, :] = pair
 
-    def ungroup(self, totals, out):
+    def ungroup(self, totals, out, base):
         tails = self.tails(totals)
         first = self.experts * self.main
         for j in range(self.blocks):
             for e in range(self.experts):
-                out[j, e * self.main:(e + 1) * self.main, :] = totals[e][j * self.main:(j + 1) * self.main]
-            out[j, first:, :] = tails[j * self.tile:(j + 1) * self.tile]
+                out[base + j, e * self.main:(e + 1) * self.main, :] = totals[e][j * self.main:(j + 1) * self.main]
+            out[base + j, first:, :] = tails[j * self.tile:(j + 1) * self.tile]
 
 
 def regroup_kernel(lay, where, x_ref, keep_ref, give_ref):
@@ -233,20 +233,22 @@
         all_ref[at, :] = value
 
     gather_rows(where, put_to, own[...], low[...], high[...], (far_a[...], far_b[...]), lay.half // rows, rows)
-    for out, weight in ((mine_ref, dm), (other_ref, do)):
+    for out, weight, base in ((mine_ref, dm, where[1] * lay.blocks), (other_ref, do, 0)):
         totals = [dot(lay.of_expert(all_ref, e), weight[e], 1, 0).astype(BF16) for e in range(lay.experts)]
-        lay.ungroup(totals, out)
+        lay.ungroup(totals, out, base)
 
 
 def expert_out_of(where, pieces, dm, do, lay):
     experts, width, feats = dm.shape
     vmem = pl.BlockSpec(memory_space=pltpu.VMEM)
-    out = jax.ShapeDtypeStruct((lay.blocks, experts * lay.main + lay.tile, feats), BF16)
+    block = (experts * lay.main + lay.tile, feats)
+    full = jax.ShapeDtypeStruct((CORES * lay.blocks, *block), BF16)
+    out = jax.ShapeDtypeStruct((lay.blocks, *block), BF16)
     return pl.pallas_call(
         functools.partial(expert_out_kernel, lay),
         in_specs=[pl.BlockSpec(memory_space=pltpu.SMEM)] + [vmem] * 7,
         out_specs=[vmem] * 3,
-        out_shape=[out, out, jax.ShapeDtypeStruct((lay.half, width), BF16)],
+        out_shape=[full, out, jax.ShapeDtypeStruct((lay.half, width), BF16)],
         name="expert_out",
     )(where, *pieces, dm, do)
 
@@ -259,28 +261,31 @@
             all_ref[i, at, :] = value
 
         gather_rows(where, put_to, own[i], low[i], high[i], (far[...],), lay.half // rows, rows)
-    for out, gw, uw in ((mine_ref, gm, um), (other_ref, go, uo)):
+    for out, gw, uw, base in ((mine_ref, gm, um, where[1] * lay.blocks), (other_ref, go, uo, 0)):
         totals = []
         for e in range(lay.experts):
             total = dot(lay.of_expert(all_ref.at[0], e), gw[e], 1, 1)
             totals.append((total + dot(lay.of_expert(all_ref.at[1], e), uw[e], 1, 1)).astype(BF16))
-        lay.ungroup(totals, out)
+        lay.ungroup(totals, out, base)
 
 
 def slot_in_of(where, pieces, gm, go, um, uo, lay):
     experts, feats, width = gm.shape
     vmem = pl.BlockSpec(memory_space=pltpu.VMEM)
-    out = jax.ShapeDtypeStruct((lay.blocks, experts * lay.main + lay.tile, feats), BF16)
+    block = (experts * lay.main + lay.tile, feats)
+    full = jax.ShapeDtypeStruct((CORES * lay.blocks, *block), BF16)
+    out = jax.ShapeDtypeStruct((lay.blocks, *block), BF16)
     return pl.pallas_call(
         functools.partial(slot_in_kernel, lay),
         in_specs=[pl.BlockSpec(memory_space=pltpu.SMEM)] + [vmem] * 9,
         out_specs=[vmem] * 3,
-        out_shape=[out, out, jax.ShapeDtypeStruct((2, lay.half, width), BF16)],
+        out_shape=[full, out, jax.ShapeDtypeStruct((2, lay.half, width), BF16)],
         name="slot_in",
     )(where, *pieces, gm, go, um, uo)
 
 
-def weight_grad_kernel(lay, a_own, a_far, b_own, b_far, out_ref, a_by, b_by):
+def weight_grad_kernel(lay, count, a_own, a_far, b_own, b_far, *refs):
+    outs, (a_by, b_by) = refs[:count], refs[count:]
     e = pl.program_id(0)
     main = pl.ds(pl.multiple_of(e * lay.per, 16), lay.per)
     at = [pl.ds(0, lay.per), pl.ds(lay.per, lay.per)]
@@ -289,29 +294,31 @@
     @pl.when(pl.program_id(1) == 0)
     def _():
         for k, ref in enumerate((a_own, a_far)):
-            a_by[at[k], :] = ref[main, :]
+            a_by[:, at[k]] = ref[main, :].T
             tail = ref[lay.start:, :]
-            a_by[rest[k], :] = jnp.where(lay.tail_of(e), tail, jnp.zeros_like(tail))
-
-    for k, ref in enumerate((b_own, b_far)):
-        b_by[at[k], :] = ref[0, main, :]
-        b_by[rest[k], :] = ref[0, lay.start:, :]
-    out_ref[0] = dot(a_by[...], b_by[...], 0, 0).astype(BF16)
-
-
-def weight_grad(a_own, a_far, b_own, b_far, i, lay):
+            a_by[:, rest[k]] = jnp.where(lay.tail_of(e), tail, jnp.zeros_like(tail)).T
+
+    for i, out in enumerate(outs):
+        for k, ref in enumerate((b_own, b_far)):
+            b_by[at[k], :] = ref[i, main, :]
+            b_by[rest[k], :] = ref[i, lay.start:, :]
+        out[0] = dot(a_by[...], b_by[...], 1, 0).astype(BF16)
+
+
+def weight_grad(a_own, a_far, b_own, b_far, lay):
     rows = 2 * (lay.per + lay.tail)
-    a_cols, b_cols = a_own.shape[1], b_own.shape[2]
+    a_cols, (count, _, b_cols) = a_own.shape[1], b_own.shape
     tile = 256
     a_spec = pl.BlockSpec(a_own.shape, lambda e, n: (0, 0))
-    b_spec = pl.BlockSpec((1, lay.half, tile), lambda e, n: (i, 0, n))
+    b_spec = pl.BlockSpec((count, lay.half, tile), lambda e, n: (0, 0, n))
+    out = pl.BlockSpec((1, a_cols, tile), lambda e, n: (e, 0, n))
     return pl.pallas_call(
-        functools.partial(weight_grad_kernel, lay),
+        functools.partial(weight_grad_kernel, lay, count),
         grid=(lay.experts, b_cols // tile),
         in_specs=[a_spec, a_spec, b_spec, b_spec],
-        out_specs=pl.BlockSpec((1, a_cols, tile), lambda e, n: (e, 0, n)),
-        out_shape=jax.ShapeDtypeStruct((lay.experts, a_cols, b_cols), BF16),
-        scratch_shapes=[pltpu.VMEM((rows, a_cols), BF16), pltpu.VMEM((rows, tile), BF16)],
+        out_specs=[out] * count,
+        out_shape=[jax.ShapeDtypeStruct((lay.experts, a_cols, b_cols), BF16)] * count,
+        scratch_shapes=[pltpu.VMEM((a_cols, rows), BF16), pltpu.VMEM((rows, tile), BF16)],
         name="weight_grad",
     )(a_own, a_far, b_own, b_far)
 
@@ -392,8 +399,8 @@
     gate_other = swap(gate_weight)
     up_other = swap(up_weight)
     down_other = swap(down_weight)
-    pairs = jnp.concatenate([expert_ids.astype(F32), route_weight], axis=1)
-    pairs_other = cross(pairs)
+    ids_other = cross(expert_ids)
+    weight_other = cross(route_weight)
     out_grad_other = cross(out_grad)
 
     block_rows = local_experts * cap
@@ -418,9 +425,7 @@
         return lax.all_to_all(a, ("y", "x"), split_axis=0, concat_axis=0, tiled=True)
 
     def both_halves(mine, other):
-        got = swap(other)
-        return jnp.concatenate(
-            [lax.select_n(core == 0, got, mine), lax.select_n(core == 0, mine, got)], axis=0)
+        return lax.dynamic_update_slice_in_dim(mine, swap(other), (1 - core) * lay.blocks, 0)
 
     recv_x = exchange(send_x)
     x_keep, x_give = regroup(where, recv_x, lay)
@@ -428,9 +433,8 @@
 
     token = jnp.arange(n_z * tok_count, dtype=jnp.int32)
     same = token[:, None] // tok_count == at[None, :] % n_z
-    pairs2 = by_plane(pairs, pairs_other)
     picker2, weight2 = routing(
-        pairs2[:, :topk].astype(jnp.int32), pairs2[:, topk:],
+        by_plane(expert_ids, ids_other), by_plane(route_weight, weight_other),
         owner_of(z_lo), rank, same, tok_count, experts_all)
     picked_g = dot(picker2, by_plane(out_grad, out_grad_other), 0, 0)
     send_g = (jnp.sum(weight2, axis=0)[:, None] * picked_g).astype(BF16)
@@ -469,10 +473,9 @@
     in_grad = dot(picker, back_in, 1, 0).astype(BF16)
 
     hidden_other = swap(hidden)
-    grad_down = weight_grad(hidden, hidden_other, g_keep[None], g_give[None], 0, lay)
+    grad_down, = weight_grad(hidden, hidden_other, g_keep[None], g_give[None], lay)
     grads_other = swap(grads)
-    grad_gate = weight_grad(x_keep, x_give, grads, grads_other, 0, lay)
-    grad_up = weight_grad(x_keep, x_give, grads, grads_other, 1, lay)
+    grad_gate, grad_up = weight_grad(x_keep, x_give, grads, grads_other, lay)
     grad_up, sum_mine = lax.optimization_barrier((grad_up, sum_mine))
     mixed = (sum_mine + from_far).astype(BF16)
     return (mixed, in_grad, grad_gate, grad_up, grad_down)

time: 247 us -> 246 us (level)
  starting transfers between devices: 69 us -> 85.5 us
  waiting for transfers between devices: 99.7 us -> 90.5 us
  other arithmetic: 12.2 us -> 7.43 us
  Pallas kernels: 50 us -> 45.7 us
    ppermute x8, starting transfers between devices: 5.66 us -> 26.7 us  [up_one(): return lax.ppermute(a, 'replica', to_up)]
    ppermute x8, waiting for transfers between devices: 29 us -> 22.1 us  [down_one(): return lax.ppermute(a, 'replica', to_down)]
    ppermute x8, starting transfers between devices: 24.3 us -> 17.4 us  [down_one(): return lax.ppermute(a, 'replica', to_down)]
    pallas_call x3 -> x2, Pallas kernels: 18.8 us -> 14.5 us  [weight_grad(): pl.pallas_call(functools.partial(weight_grad_kernel, lay, count), grid=(l...]
    ppermute x3 -> x4, starting transfers between devices: 2.97 us -> 5.63 us  [cross(): return lax.ppermute(a, 'z_lo', to_plane)]
    ppermute x3 -> x4, waiting for transfers between devices: 14.6 us -> 15.3 us  [cross(): return lax.ppermute(a, 'z_lo', to_plane)]
  transfers between devices with their start and end apart: 32 -> 33, of which waited for: 13 -> 16; matrix products, arithmetic and copies ran while one was open for 6% -> 7% of each run, Pallas kernels for 20% -> 19%
where the time goes in v1:
time: 246 us; the launch traced here: 245 us
  waiting for transfers between devices  90.5 us (37%)
  starting transfers between devices  85.5 us (35%)
  Pallas kernels  45.7 us (19%)
  matrix products  9.48 us (4%)
  other arithmetic  7.43 us (3%)
  local copies, waits for them, and re-layouts  5.91 us (2%)
    ppermute x8, waiting for transfers between devices, up_one(): return lax.ppermute(a, 'replica', to_up)  38.5 us
    ppermute x8, starting transfers between devices, up_one(): return lax.ppermute(a, 'replica', to_up)  26.7 us
    ppermute x8, waiting for transfers between devices, down_one(): return lax.ppermute(a, 'replica', to_down)  22.1 us
    ppermute x8, starting transfers between devices, down_one(): return lax.ppermute(a, 'replica', to_down)  17.4 us
    ppermute x4, waiting for transfers between devices, cross(): return lax.ppermute(a, 'z_lo', to_plane)  15.3 us
    pallas_call x2, Pallas kernels, weight_grad(): pl.pallas_call(functools.partial(weight_grad_kernel, lay, count), grid=(l...  14.5 us
    all_to_all x2, starting transfers between devices, exchange(): lax.all_to_all(a, ('y', 'x', 'z_lo'), split_axis=0, concat_axis=0, tiled=...  12.7 us
    all_to_all x2, starting transfers between devices, exchange_plane(): lax.all_to_all(a, ('y', 'x'), split_axis=0, concat_axis=0, tiled=True)  11.7 us
  transfers between devices with their start and end apart: 33, of which 16 were waited for; matrix products, arithmetic and copies ran while one was open for 7% of the time, Pallas kernels for 19%

profile of v1, /device:TPU:1, one launch (start us, length us, event | category | flops | bytes accessed | tf_op | source)
XLA Modules:
  0.0 245.5 jit_solution(16244934854260895880)
XLA Ops:
  6.2 7.2 %all-to-all-start = ((bf16[32,40,512]{2,1,0:T(8,128)(2,1)}), bf16[32,40,512]{2,1,0:T(8,128)(2,1)S(1)}, u32[]{:S(2)}, u32[]{:S(2)}) async-start(bf16[32,40,512]{2,1,0:T(8,128)(2,1)} %bitcast.2), calls=%async_computation | async-start | bytes 2621440 | tf_op jit(solution)/shard_map/all_to_all | solution.py:421
  15.1 13.4 %collective-permute-done.1 = f32[128,8]{0,1:T(8,128)S(1)} collective-permute-done((f32[128,8]{0,1:T(8,128)S(1)}, f32[128,8]{0,1:T(8,128)S(1)}, u32[]{:S(2)}, u32[]{:S(2)}) %collective-permute-start.1) | collective-permute-done | bytes 4128 | tf_op jit(solution)/shard_map/ppermute | solution.py:393
  34.9 6.7 %all-to-all-start.1 = ((bf16[16,80,512]{2,1,0:T(8,128)(2,1)}), bf16[16,80,512]{2,1,0:T(8,128)(2,1)}, u32[]{:S(2)}, u32[]{:S(2)}) async-start(bf16[16,80,512]{2,1,0:T(8,128)(2,1)} %bitcast.50), calls=%async_computation.1 | async-start | bytes 2621440 | tf_op jit(solution)/shard_map/all_to_all | solution.py:425
  48.4 10.6 %all-to-all-done.1 = bf16[16,80,512]{2,1,0:T(8,128)(2,1)} async-done(((bf16[16,80,512]{2,1,0:T(8,128)(2,1)}), bf16[16,80,512]{2,1,0:T(8,128)(2,1)}, u32[]{:S(2)}, u32[]{:S(2)}) %all-to-all-start.1) | async-done | bytes 1310752 | tf_op jit(solution)/shard_map/all_to_all | solution.py:425
  61.5 4.4 %collective-permute-start.3 = (bf16[640,512]{1,0:T(8,128)(2,1)}, bf16[640,512]{1,0:T(8,128)(2,1)}, u32[]{:S(2)}, u32[]{:S(2)}) collective-permute-start(bf16[640,512]{1,0:T(8,128)(2,1)} %get-tuple-element.32), channel_id=1, source_target_pairs={{0,1},{1,0},{2,3},{3,2},{4,5},{5,4},{6,7},{7,6},{8,9},{9,8},{10,11... | collective-permute-start | bytes 1966088 | tf_op jit(solution)/shard_map/ppermute | solution.py:370
  65.8 7.8 %gate_up.1 = (bf16[2,160,768]{2,1,0:T(8,128)(2,1)}, bf16[2,160,768]{2,1,0:T(8,128)(2,1)}, f32[2,160,768]{2,1,0:T(8,128)}, f32[2,160,768]{2,1,0:T(8,128)}) custom-call(s32[2]{0:T(128)} %pad_add_fusion.1.where, bf16[640,512]{1,0:T(8,128)(2,1)} %get-tuple-element.29.x_ref.a_own, bf16[640,512]{1,0:T(8,128)(2,1)} %collective-permute-done.9.other_ref, ...), custom_call_target="tpu_custom_call" | custom-call | tf_op jit(solution)/shard_map/gate_up/pallas_call | solution.py:125
  79.3 5.9 %hidden_grad.1 = (bf16[2,80,768]{2,1,0:T(8,128)(2,1)}, bf16[2,80,768]{2,1,0:T(8,128)(2,1)}, f32[2,80,768]{2,1,0:T(8,128)}, f32[2,80,768]{2,1,0:T(8,128)}) custom-call(s32[2]{0:T(128)} %pad_add_fusion.1.where, bf16[640,512]{1,0:T(8,128)(2,1)} %get-tuple-element.31.g_ref, bf16[640,512]{1,0:T(8,128)(2,1)} %collective-permute-done.3.other_ref, ...), custom_call_target="tpu_custom_call" | custom-call | tf_op jit(solution)/shard_map/hidden_grad/pallas_call | solution.py:189
  89.0 23.4 %collective-permute-done.6 = bf16[2,80,768]{2,1,0:T(8,128)(2,1)S(1)} collective-permute-done((bf16[2,80,768]{2,1,0:T(8,128)(2,1)}, bf16[2,80,768]{2,1,0:T(8,128)(2,1)S(1)}, u32[]{:S(2)}, u32[]{:S(2)}) %collective-permute-start.6) | collective-permute-done | bytes 245792 | tf_op jit(solution)/shard_map/ppermute | solution.py:373
  114.5 3.4 %collective-permute-start.7 = (bf16[80,768]{1,0:T(8,128)(2,1)S(1)}, bf16[80,768]{1,0:T(8,128)(2,1)S(1)}, u32[]{:S(2)}, u32[]{:S(2)}) collective-permute-start(bf16[80,768]{1,0:T(8,128)(2,1)S(1)} %get-tuple-element.64), channel_id=1, source_target_pairs={{0,2},{1,3},{2,4},{3,5},{4,6},{5,7},{6,0},{7,1},{8,10},{9,11},{10,... | collective-permute-start | bytes 368648 | tf_op jit(solution)/shard_map/ppermute | solution.py:373
  123.9 5.8 %collective-permute-done.15 = bf16[160,768]{1,0:T(8,128)(2,1)S(1)} collective-permute-done((bf16[160,768]{1,0:T(8,128)(2,1)S(1)}, bf16[160,768]{1,0:T(8,128)(2,1)S(1)}, u32[]{:S(2)}, u32[]{:S(2)}) %collective-permute-start.15) | collective-permute-done | bytes 245792 | tf_op jit(solution)/shard_map/ppermute | solution.py:376
  138.0 8.9 %collective-permute-done.21.low = bf16[160,768]{1,0:T(8,128)(2,1)S(1)} collective-permute-done((bf16[160,768]{1,0:T(8,128)(2,1)S(1)}, bf16[160,768]{1,0:T(8,128)(2,1)S(1)}, u32[]{:S(2)}, u32[]{:S(2)}) %collective-permute-start.21) | collective-permute-done | bytes 245792 | tf_op jit(solution)/shard_map/ppermute | solution.py:373
  146.9 7.6 %collective-permute-start.23 = (bf16[80,768]{1,0:T(8,128)(2,1)S(1)}, bf16[80,768]{1,0:T(8,128)(2,1)S(1)}, u32[]{:S(2)}, u32[]{:S(2)}) collective-permute-start(bf16[80,768]{1,0:T(8,128)(2,1)S(1)} %slice.102), channel_id=1, source_target_pairs={{0,2},{1,3},{2,4},{3,5},{4,6},{5,7},{6,0},{7,1},{8,10},{9,11},{10,... | collective-permute-start | bytes 368648 | tf_op jit(solution)/shard_map/ppermute | solution.py:373
  155.3 5.8 %collective-permute-start.16 = (bf16[2,160,768]{2,1,0:T(8,128)(2,1)S(1)}, bf16[2,160,768]{2,1,0:T(8,128)(2,1)S(1)}, u32[]{:S(2)}, u32[]{:S(2)}) collective-permute-start(bf16[2,160,768]{2,1,0:T(8,128)(2,1)S(1)} %pad_maximum_fusion.1.own), channel_id=1, source_target_pairs={{0,2},{1,3},{2,4},{3,5},{4,6},{5,7},{6,0},{7,1},{8,10},{9,11},{10,... | collective-permute-start | bytes 1474568 | tf_op jit(solution)/shard_map/ppermute | solution.py:373
  162.8 4.9 %expert_out.1 = (bf16[32,40,512]{2,1,0:T(8,128)(2,1)}, bf16[16,40,512]{2,1,0:T(8,128)(2,1)}, bf16[640,768]{1,0:T(8,128)(2,1)}) custom-call(s32[2]{0:T(128)} %pad_add_fusion.1.where, bf16[160,768]{1,0:T(8,128)(2,1)} %copy-done.7, bf16[160,768]{1,0:T(8,128)(2,1)} %copy-done.8, bf16[160,768]{1,0:T(8,128)(2,1)} %copy-done.9, bf16[80,768]{1,0:T(8,128)(2,1)} %copy-done.13, ...), custom_call_target="tpu_custom_call" | custom-call | tf_op jit(solution)/shard_map/expert_out/pallas_call | solution.py:247
  169.8 4.5 %collective-permute-start.17 = (bf16[2,160,768]{2,1,0:T(8,128)(2,1)S(1)}, bf16[2,160,768]{2,1,0:T(8,128)(2,1)}, u32[]{:S(2)}, u32[]{:S(2)}) collective-permute-start(bf16[2,160,768]{2,1,0:T(8,128)(2,1)S(1)} %pad_maximum_fusion.1.own), channel_id=1, source_target_pairs={{0,6},{1,7},{2,0},{3,1},{4,2},{5,3},{6,4},{7,5},{8,14},{9,15},{10,... | collective-permute-start | bytes 1474568 | tf_op jit(solution)/shard_map/ppermute | solution.py:376
  176.3 3.1 %collective-permute-start.18 = (bf16[160,768]{1,0:T(8,128)(2,1)}, bf16[160,768]{1,0:T(8,128)(2,1)}, u32[]{:S(2)}, u32[]{:S(2)}) collective-permute-start(bf16[160,768]{1,0:T(8,128)(2,1)} %slice_bitcast_fusion.1), channel_id=1, source_target_pairs={{0,2},{1,3},{2,4},{3,5},{4,6},{5,7},{6,0},{7,1},{8,10},{9,11},{10,... | collective-permute-start | bytes 737288 | tf_op jit(solution)/shard_map/ppermute | solution.py:373
  180.2 5.0 %all-to-all-start.2 = ((bf16[16,80,512]{2,1,0:T(8,128)(2,1)}), bf16[16,80,512]{2,1,0:T(8,128)(2,1)S(1)}, u32[]{:S(2)}, u32[]{:S(2)}) async-start(bf16[16,80,512]{2,1,0:T(8,128)(2,1)} %bitcast.51), calls=%async_computation.2 | async-start | bytes 2621440 | tf_op jit(solution)/shard_map/all_to_all | solution.py:425
  185.2 5.2 %collective-permute-done.17.high = bf16[2,160,768]{2,1,0:T(8,128)(2,1)} collective-permute-done((bf16[2,160,768]{2,1,0:T(8,128)(2,1)S(1)}, bf16[2,160,768]{2,1,0:T(8,128)(2,1)}, u32[]{:S(2)}, u32[]{:S(2)}) %collective-permute-start.17) | collective-permute-done | bytes 491552 | tf_op jit(solution)/shard_map/ppermute | solution.py:376
  191.4 3.6 %collective-permute-start.19 = (bf16[160,768]{1,0:T(8,128)(2,1)S(1)}, bf16[160,768]{1,0:T(8,128)(2,1)S(1)}, u32[]{:S(2)}, u32[]{:S(2)}) collective-permute-start(bf16[160,768]{1,0:T(8,128)(2,1)S(1)} %slice_bitcast_fusion), channel_id=1, source_target_pairs={{0,6},{1,7},{2,0},{3,1},{4,2},{5,3},{6,4},{7,5},{8,14},{9,15},{10,... | collective-permute-start | bytes 737288 | tf_op jit(solution)/shard_map/ppermute | solution.py:376
  195.0 8.5 %collective-permute-done.19.far_u = bf16[160,768]{1,0:T(8,128)(2,1)S(1)} collective-permute-done((bf16[160,768]{1,0:T(8,128)(2,1)S(1)}, bf16[160,768]{1,0:T(8,128)(2,1)S(1)}, u32[]{:S(2)}, u32[]{:S(2)}) %collective-permute-start.19) | collective-permute-done | bytes 245792 | tf_op jit(solution)/shard_map/ppermute | solution.py:376
  204.3 7.8 %slot_in.1 = (bf16[32,40,512]{2,1,0:T(8,128)(2,1)}, bf16[16,40,512]{2,1,0:T(8,128)(2,1)}, bf16[2,640,768]{2,1,0:T(8,128)(2,1)}) custom-call(s32[2]{0:T(128)} %pad_add_fusion.1.where, bf16[2,160,768]{2,1,0:T(8,128)(2,1)} %copy-done.3, bf16[2,160,768]{2,1,0:T(8,128)(2,1)} %copy-done.4, bf16[2,160,768]{2,1,0:T(8,128)(2,1)} %collective-permute-done.17.high, ...), custom_call_target="tpu_custom_call" | custom-call | tf_op jit(solution)/shard_map/slot_in/pallas_call | solution.py:278
  215.3 5.5 %all-to-all-start.3 = ((bf16[32,40,512]{2,1,0:T(8,128)(2,1)}), bf16[32,40,512]{2,1,0:T(8,128)(2,1)}, u32[]{:S(2)}, u32[]{:S(2)}) async-start(bf16[32,40,512]{2,1,0:T(8,128)(2,1)} %constant_dynamic-update-slice_fusion), calls=%async_computation.3 | async-start | bytes 2621440 | tf_op jit(solution)/shard_map/all_to_all | solution.py:421
  226.9 5.9 %weight_grad.3 = bf16[2,768,512]{2,1,0:T(8,128)(2,1)} custom-call(bf16[640,768]{1,0:T(8,128)(2,1)} %get-tuple-element.52.a_own, bf16[640,768]{1,0:T(8,128)(2,1)} %collective-permute-done.28.a_far, bf16[1,640,512]{2,1,0:T(8,128)(2,1)} %bitcast.49, bf16[1,640,512]{2,1,0:T(8,128)(2,1)} %bitcast.52), custom_call_target="tpu_custom_call" | custom-call | tf_op jit(solution)/shard_map/weight_grad/pallas_call | solution.py:315
  232.8 8.6 %weight_grad.2 = (bf16[2,512,768]{2,1,0:T(8,128)(2,1)}, bf16[2,512,768]{2,1,0:T(8,128)(2,1)}) custom-call(bf16[640,512]{1,0:T(8,128)(2,1)} %get-tuple-element.29.x_ref.a_own, bf16[640,512]{1,0:T(8,128)(2,1)} %get-tuple-element.30.a_far, bf16[2,640,768]{2,1,0:T(8,128)(2,1)} %get-tuple-element.43.b_own, bf16[2,640,768]{2,1,0:T(8,128)(2,1)} %collective-permute-done.20.b_far), custom_call_target="tpu_custom_call" | custom-call | tf_op jit(solution)/shard_map/weight_grad/pallas_call | solution.py:315
  (124 shorter events, 71.2 us)
Async XLA Ops:
  0.6 14.4 %collective-permute-start = (s32[128,8]{0,1:T(8,128)}, s32[128,8]{0,1:T(8,128)S(1)}, u32[]{:S(2)}, u32[]{:S(2)}) collective-permute-start(s32[128,8]{0,1:T(8,128)} %param.9), channel_id=1, source_target_pairs={{0,32},{32,0},{1,33},{33,1},{2,34},{34,2},{3,35},{35,3},{4,36},{36... | collective-permute-start | bytes 12296 | tf_op jit(solution)/shard_map/ppermute | solution.py:393
  6.2 27.7 %all-to-all-start = ((bf16[32,40,512]{2,1,0:T(8,128)(2,1)}), bf16[32,40,512]{2,1,0:T(8,128)(2,1)S(1)}, u32[]{:S(2)}, u32[]{:S(2)}) async-start(bf16[32,40,512]{2,1,0:T(8,128)(2,1)} %bitcast.2), calls=%async_computation | async-start | bytes 2621440 | tf_op jit(solution)/shard_map/all_to_all | solution.py:421
  13.4 15.1 %collective-permute-start.1 = (f32[128,8]{0,1:T(8,128)S(1)}, f32[128,8]{0,1:T(8,128)S(1)}, u32[]{:S(2)}, u32[]{:S(2)}) collective-permute-start(f32[128,8]{0,1:T(8,128)S(1)} %copy-done.15), channel_id=1, source_target_pairs={{0,32},{32,0},{1,33},{33,1},{2,34},{34,2},{3,35},{35,3},{4,36},{36... | collective-permute-start | bytes 12296 | tf_op jit(solution)/shard_map/ppermute | solution.py:393
  14.7 16.5 %collective-permute-start.2 = (bf16[128,512]{1,0:T(8,128)(2,1)S(1)}, bf16[128,512]{1,0:T(8,128)(2,1)}, u32[]{:S(2)}, u32[]{:S(2)}) collective-permute-start(bf16[128,512]{1,0:T(8,128)(2,1)S(1)} %copy-done.12), channel_id=1, source_target_pairs={{0,32},{32,0},{1,33},{33,1},{2,34},{34,2},{3,35},{35,3},{4,36},{36... | collective-permute-start | bytes 393224 | tf_op jit(solution)/shard_map/ppermute | solution.py:393
  34.9 24.1 %all-to-all-start.1 = ((bf16[16,80,512]{2,1,0:T(8,128)(2,1)}), bf16[16,80,512]{2,1,0:T(8,128)(2,1)}, u32[]{:S(2)}, u32[]{:S(2)}) async-start(bf16[16,80,512]{2,1,0:T(8,128)(2,1)} %bitcast.50), calls=%async_computation.1 | async-start | bytes 2621440 | tf_op jit(solution)/shard_map/all_to_all | solution.py:425
  41.6 24.2 %collective-permute-start.10 = (bf16[2,512,768]{2,1,0:T(8,128)(2,1)}, bf16[2,512,768]{2,1,0:T(8,128)(2,1)}, u32[]{:S(2)}, u32[]{:S(2)}) collective-permute-start(bf16[2,512,768]{2,1,0:T(8,128)(2,1)} %gm.3), channel_id=1, source_target_pairs={{0,1},{1,0},{2,3},{3,2},{4,5},{5,4},{6,7},{7,6},{8,9},{9,8},{10,11... | collective-permute-start | bytes 4718600 | tf_op jit(solution)/shard_map/ppermute | solution.py:370
  44.7 21.2 %collective-permute-start.11 = (bf16[2,512,768]{2,1,0:T(8,128)(2,1)}, bf16[2,512,768]{2,1,0:T(8,128)(2,1)}, u32[]{:S(2)}, u32[]{:S(2)}) collective-permute-start(bf16[2,512,768]{2,1,0:T(8,128)(2,1)} %um.3), channel_id=1, source_target_pairs={{0,1},{1,0},{2,3},{3,2},{4,5},{5,4},{6,7},{7,6},{8,9},{9,8},{10,11... | collective-permute-start | bytes 4718600 | tf_op jit(solution)/shard_map/ppermute | solution.py:370
  44.8 34.5 %collective-permute-start.4 = (bf16[2,768,512]{2,1,0:T(8,128)(2,1)S(1)}, bf16[2,768,512]{2,1,0:T(8,128)(2,1)}, u32[]{:S(2)}, u32[]{:S(2)}) collective-permute-start(bf16[2,768,512]{2,1,0:T(8,128)(2,1)S(1)} %copy-done.1), channel_id=1, source_target_pairs={{0,1},{1,0},{2,3},{3,2},{4,5},{5,4},{6,7},{7,6},{8,9},{9,8},{10,11... | collective-permute-start | bytes 4718600 | tf_op jit(solution)/shard_map/ppermute | solution.py:370
  48.3 17.5 %collective-permute-start.9 = (bf16[640,512]{1,0:T(8,128)(2,1)}, bf16[640,512]{1,0:T(8,128)(2,1)}, u32[]{:S(2)}, u32[]{:S(2)}) collective-permute-start(bf16[640,512]{1,0:T(8,128)(2,1)} %get-tuple-element.30.a_far), channel_id=1, source_target_pairs={{0,1},{1,0},{2,3},{3,2},{4,5},{5,4},{6,7},{7,6},{8,9},{9,8},{10,11... | collective-permute-start | bytes 1966088 | tf_op jit(solution)/shard_map/ppermute | solution.py:370
  61.5 17.8 %collective-permute-start.3 = (bf16[640,512]{1,0:T(8,128)(2,1)}, bf16[640,512]{1,0:T(8,128)(2,1)}, u32[]{:S(2)}, u32[]{:S(2)}) collective-permute-start(bf16[640,512]{1,0:T(8,128)(2,1)} %get-tuple-element.32), channel_id=1, source_target_pairs={{0,1},{1,0},{2,3},{3,2},{4,5},{5,4},{6,7},{7,6},{8,9},{9,8},{10,11... | collective-permute-start | bytes 1966088 | tf_op jit(solution)/shard_map/ppermute | solution.py:370
  73.6 44.6 %collective-permute-start.13 = (bf16[2,160,768]{2,1,0:T(8,128)(2,1)}, bf16[2,160,768]{2,1,0:T(8,128)(2,1)}, u32[]{:S(2)}, u32[]{:S(2)}) collective-permute-start(bf16[2,160,768]{2,1,0:T(8,128)(2,1)} %get-tuple-element.40), channel_id=1, source_target_pairs={{0,2},{1,3},{2,4},{3,5},{4,6},{5,7},{6,0},{7,1},{8,10},{9,11},{10,... | collective-permute-start | bytes 1474568 | tf_op jit(solution)/shard_map/ppermute | solution.py:373
  76.6 41.6 %collective-permute-start.12 = (bf16[2,160,768]{2,1,0:T(8,128)(2,1)}, bf16[2,160,768]{2,1,0:T(8,128)(2,1)}, u32[]{:S(2)}, u32[]{:S(2)}) collective-permute-start(bf16[2,160,768]{2,1,0:T(8,128)(2,1)} %get-tuple-element.38), channel_id=1, source_target_pairs={{0,6},{1,7},{2,0},{3,1},{4,2},{5,3},{6,4},{7,5},{8,14},{9,15},{10,... | collective-permute-start | bytes 1474568 | tf_op jit(solution)/shard_map/ppermute | solution.py:376
  85.2 27.2 %collective-permute-start.6 = (bf16[2,80,768]{2,1,0:T(8,128)(2,1)}, bf16[2,80,768]{2,1,0:T(8,128)(2,1)S(1)}, u32[]{:S(2)}, u32[]{:S(2)}) collective-permute-start(bf16[2,80,768]{2,1,0:T(8,128)(2,1)} %get-tuple-element.36), channel_id=1, source_target_pairs={{0,2},{1,3},{2,4},{3,5},{4,6},{5,7},{6,0},{7,1},{8,10},{9,11},{10,... | collective-permute-start | bytes 737288 | tf_op jit(solution)/shard_map/ppermute | solution.py:373
  86.5 26.8 %collective-permute-start.5 = (bf16[2,80,768]{2,1,0:T(8,128)(2,1)}, bf16[2,80,768]{2,1,0:T(8,128)(2,1)S(1)}, u32[]{:S(2)}, u32[]{:S(2)}) collective-permute-start(bf16[2,80,768]{2,1,0:T(8,128)(2,1)} %get-tuple-element.34), channel_id=1, source_target_pairs={{0,6},{1,7},{2,0},{3,1},{4,2},{5,3},{6,4},{7,5},{8,14},{9,15},{10,... | collective-permute-start | bytes 737288 | tf_op jit(solution)/shard_map/ppermute | solution.py:376
  134.1 12.8 %collective-permute-start.21 = (bf16[160,768]{1,0:T(8,128)(2,1)S(1)}, bf16[160,768]{1,0:T(8,128)(2,1)S(1)}, u32[]{:S(2)}, u32[]{:S(2)}) collective-permute-start(bf16[160,768]{1,0:T(8,128)(2,1)S(1)} %get-tuple-element.53.own), channel_id=1, source_target_pairs={{0,2},{1,3},{2,4},{3,5},{4,6},{5,7},{6,0},{7,1},{8,10},{9,11},{10,... | collective-permute-start | bytes 737288 | tf_op jit(solution)/shard_map/ppermute | solution.py:373
  135.3 19.2 %collective-permute-start.22 = (bf16[160,768]{1,0:T(8,128)(2,1)S(1)}, bf16[160,768]{1,0:T(8,128)(2,1)S(1)}, u32[]{:S(2)}, u32[]{:S(2)}) collective-permute-start(bf16[160,768]{1,0:T(8,128)(2,1)S(1)} %get-tuple-element.53.own), channel_id=1, source_target_pairs={{0,6},{1,7},{2,0},{3,1},{4,2},{5,3},{6,4},{7,5},{8,14},{9,15},{10,... | collective-permute-start | bytes 737288 | tf_op jit(solution)/shard_map/ppermute | solution.py:376
  146.9 14.3 %collective-permute-start.23 = (bf16[80,768]{1,0:T(8,128)(2,1)S(1)}, bf16[80,768]{1,0:T(8,128)(2,1)S(1)}, u32[]{:S(2)}, u32[]{:S(2)}) collective-permute-start(bf16[80,768]{1,0:T(8,128)(2,1)S(1)} %slice.102), channel_id=1, source_target_pairs={{0,2},{1,3},{2,4},{3,5},{4,6},{5,7},{6,0},{7,1},{8,10},{9,11},{10,... | collective-permute-start | bytes 368648 | tf_op jit(solution)/shard_map/ppermute | solution.py:373
  155.3 20.2 %collective-permute-start.16 = (bf16[2,160,768]{2,1,0:T(8,128)(2,1)S(1)}, bf16[2,160,768]{2,1,0:T(8,128)(2,1)S(1)}, u32[]{:S(2)}, u32[]{:S(2)}) collective-permute-start(bf16[2,160,768]{2,1,0:T(8,128)(2,1)S(1)} %pad_maximum_fusion.1.own), channel_id=1, source_target_pairs={{0,2},{1,3},{2,4},{3,5},{4,6},{5,7},{6,0},{7,1},{8,10},{9,11},{10,... | collective-permute-start | bytes 1474568 | tf_op jit(solution)/shard_map/ppermute | solution.py:373
  169.8 20.7 %collective-permute-start.17 = (bf16[2,160,768]{2,1,0:T(8,128)(2,1)S(1)}, bf16[2,160,768]{2,1,0:T(8,128)(2,1)}, u32[]{:S(2)}, u32[]{:S(2)}) collective-permute-start(bf16[2,160,768]{2,1,0:T(8,128)(2,1)S(1)} %pad_maximum_fusion.1.own), channel_id=1, source_target_pairs={{0,6},{1,7},{2,0},{3,1},{4,2},{5,3},{6,4},{7,5},{8,14},{9,15},{10,... | collective-permute-start | bytes 1474568 | tf_op jit(solution)/shard_map/ppermute | solution.py:376
  176.3 18.8 %collective-permute-start.18 = (bf16[160,768]{1,0:T(8,128)(2,1)}, bf16[160,768]{1,0:T(8,128)(2,1)}, u32[]{:S(2)}, u32[]{:S(2)}) collective-permute-start(bf16[160,768]{1,0:T(8,128)(2,1)} %slice_bitcast_fusion.1), channel_id=1, source_target_pairs={{0,2},{1,3},{2,4},{3,5},{4,6},{5,7},{6,0},{7,1},{8,10},{9,11},{10,... | collective-permute-start | bytes 737288 | tf_op jit(solution)/shard_map/ppermute | solution.py:373
  180.2 35.1 %all-to-all-start.2 = ((bf16[16,80,512]{2,1,0:T(8,128)(2,1)}), bf16[16,80,512]{2,1,0:T(8,128)(2,1)S(1)}, u32[]{:S(2)}, u32[]{:S(2)}) async-start(bf16[16,80,512]{2,1,0:T(8,128)(2,1)} %bitcast.51), calls=%async_computation.2 | async-start | bytes 2621440 | tf_op jit(solution)/shard_map/all_to_all | solution.py:425
  191.4 12.2 %collective-permute-start.19 = (bf16[160,768]{1,0:T(8,128)(2,1)S(1)}, bf16[160,768]{1,0:T(8,128)(2,1)S(1)}, u32[]{:S(2)}, u32[]{:S(2)}) collective-permute-start(bf16[160,768]{1,0:T(8,128)(2,1)S(1)} %slice_bitcast_fusion), channel_id=1, source_target_pairs={{0,6},{1,7},{2,0},{3,1},{4,2},{5,3},{6,4},{7,5},{8,14},{9,15},{10,... | collective-permute-start | bytes 737288 | tf_op jit(solution)/shard_map/ppermute | solution.py:376
  215.3 27.8 %all-to-all-start.3 = ((bf16[32,40,512]{2,1,0:T(8,128)(2,1)}), bf16[32,40,512]{2,1,0:T(8,128)(2,1)}, u32[]{:S(2)}, u32[]{:S(2)}) async-start(bf16[32,40,512]{2,1,0:T(8,128)(2,1)} %constant_dynamic-update-slice_fusion), calls=%async_computation.3 | async-start | bytes 2621440 | tf_op jit(solution)/shard_map/all_to_all | solution.py:421
  223.3 19.2 %collective-permute-start.26 = (f32[128,512]{1,0:T(8,128)S(1)}, f32[128,512]{1,0:T(8,128)S(1)}, u32[]{:S(2)}, u32[]{:S(2)}) collective-permute-start(f32[128,512]{1,0:T(8,128)S(1)} %get-tuple-element.60), channel_id=1, source_target_pairs={{0,32},{32,0},{1,33},{33,1},{2,34},{34,2},{3,35},{35,3},{4,36},{36... | collective-permute-start | bytes 786440 | tf_op jit(solution)/shard_map/ppermute | solution.py:393
  (25 other events, 225.8 us)

commit v2 on v1

--- a/solution.py
+++ b/solution.py
@@ -455,9 +455,12 @@
         where, (own, low, high, far_a, far_b), down_weight, down_other, lay)
     expert_out = both_halves(mine, other)
     returned = exchange_plane(expert_out).reshape(slots, feats)
-    sums = weighted_sum(weight2, returned).reshape(n_z, tok_count, feats)
-    sum_mine = lax.select_n(z_lo == 0, sums[1], sums[0])
-    from_far = cross(lax.select_n(z_lo == 0, sums[0], sums[1]))
+    first, second = weight2[:tok_count], weight2[tok_count:]
+    weight_mine = lax.select_n(z_lo == 0, second, first)
+    weight_far = lax.select_n(z_lo == 0, first, second)
+    weight_mine, weight_far = lax.optimization_barrier((weight_mine, weight_far))
+    from_far = cross(weighted_sum(weight_far, returned))
+    sum_mine = weighted_sum(weight_mine, returned)
 
     gate, up = lax.optimization_barrier((gate, up))
     sig = jax.nn.sigmoid(gate)

time: 246 us -> 249 us (1.012)
  starting transfers between devices: 85.5 us -> 82.9 us
  waiting for transfers between devices: 90.5 us -> 93.1 us
    ppermute x9, starting transfers between devices: 11.5 us -> 25.6 us  [swap(): return lax.ppermute(a, 'replica', to_swap)]
    ppermute x8, waiting for transfers between devices: 22.1 us -> 34.6 us  [down_one(): return lax.ppermute(a, 'replica', to_down)]
    ppermute x8, starting transfers between devices: 26.7 us -> 16.7 us  [up_one(): return lax.ppermute(a, 'replica', to_up)]
    ppermute x8, waiting for transfers between devices: 38.5 us -> 32.6 us  [up_one(): return lax.ppermute(a, 'replica', to_up)]
    ppermute x8, starting transfers between devices: 17.4 us -> 12.7 us  [down_one(): return lax.ppermute(a, 'replica', to_down)]
    dot_general x11 -> x14, matrix products: 9.48 us -> 11.1 us  [dot(): lax.dot_general(a, b, (((ca,), (cb,)), ((), ())), preferred_element_type=...]
  transfers between devices with their start and end apart: 33 -> 33, of which waited for: 16 -> 15; matrix products, arithmetic and copies ran while one was open for 7% -> 7% of each run, Pallas kernels for 19% -> 18%
where the time goes in v2:
time: 249 us; the launch traced here: 248 us
  waiting for transfers between devices  93.1 us (37%)
  starting transfers between devices  82.9 us (33%)
  Pallas kernels  45.7 us (18%)
  matrix products  11.1 us (4%)
  other arithmetic  7.88 us (3%)
  local copies, waits for them, and re-layouts  6.21 us (2%)
    ppermute x8, waiting for transfers between devices, down_one(): return lax.ppermute(a, 'replica', to_down)  34.6 us
    ppermute x8, waiting for transfers between devices, up_one(): return lax.ppermute(a, 'replica', to_up)  32.6 us
    ppermute x9, starting transfers between devices, swap(): return lax.ppermute(a, 'replica', to_swap)  25.6 us
    ppermute x8, starting transfers between devices, up_one(): return lax.ppermute(a, 'replica', to_up)  16.7 us
    ppermute x4, waiting for transfers between devices, cross(): return lax.ppermute(a, 'z_lo', to_plane)  14.9 us
    pallas_call x2, Pallas kernels, weight_grad(): pl.pallas_call(functools.partial(weight_grad_kernel, lay, count), grid=(l...  14.5 us
    ppermute x8, starting transfers between devices, down_one(): return lax.ppermute(a, 'replica', to_down)  12.7 us
    all_to_all x2, starting transfers between devices, exchange(): lax.all_to_all(a, ('y', 'x', 'z_lo'), split_axis=0, concat_axis=0, tiled=...  11.9 us
  transfers between devices with their start and end apart: 33, of which 15 were waited for; matrix products, arithmetic and copies ran while one was open for 7% of the time, Pallas kernels for 18%

profile of v2, /device:TPU:1, one launch (start us, length us, event | category | flops | bytes accessed | tf_op | source)
XLA Modules:
  0.0 247.8 jit_solution(1919968909675180620)
XLA Ops:
  6.2 7.2 %all-to-all-start = ((bf16[32,40,512]{2,1,0:T(8,128)(2,1)}), bf16[32,40,512]{2,1,0:T(8,128)(2,1)S(1)}, u32[]{:S(2)}, u32[]{:S(2)}) async-start(bf16[32,40,512]{2,1,0:T(8,128)(2,1)} %bitcast.2), calls=%async_computation | async-start | bytes 2621440 | tf_op jit(solution)/shard_map/all_to_all | solution.py:421
  15.1 13.4 %collective-permute-done.1 = f32[128,8]{0,1:T(8,128)S(1)} collective-permute-done((f32[128,8]{0,1:T(8,128)S(1)}, f32[128,8]{0,1:T(8,128)S(1)}, u32[]{:S(2)}, u32[]{:S(2)}) %collective-permute-start.1) | collective-permute-done | bytes 4128 | tf_op jit(solution)/shard_map/ppermute | solution.py:393
  34.3 6.7 %all-to-all-start.1 = ((bf16[16,80,512]{2,1,0:T(8,128)(2,1)}), bf16[16,80,512]{2,1,0:T(8,128)(2,1)}, u32[]{:S(2)}, u32[]{:S(2)}) async-start(bf16[16,80,512]{2,1,0:T(8,128)(2,1)} %bitcast.3), calls=%async_computation.1 | async-start | bytes 2621440 | tf_op jit(solution)/shard_map/all_to_all | solution.py:425
  41.0 3.8 %collective-permute-start.10 = (bf16[2,512,768]{2,1,0:T(8,128)(2,1)}, bf16[2,512,768]{2,1,0:T(8,128)(2,1)}, u32[]{:S(2)}, u32[]{:S(2)}) collective-permute-start(bf16[2,512,768]{2,1,0:T(8,128)(2,1)} %gm.3), channel_id=1, source_target_pairs={{0,1},{1,0},{2,3},{3,2},{4,5},{5,4},{6,7},{7,6},{8,9},{9,8},{10,11... | collective-permute-start | bytes 4718600 | tf_op jit(solution)/shard_map/ppermute | solution.py:370
  48.6 9.1 %all-to-all-done.1 = bf16[16,80,512]{2,1,0:T(8,128)(2,1)} async-done(((bf16[16,80,512]{2,1,0:T(8,128)(2,1)}), bf16[16,80,512]{2,1,0:T(8,128)(2,1)}, u32[]{:S(2)}, u32[]{:S(2)}) %all-to-all-start.1) | async-done | bytes 1310752 | tf_op jit(solution)/shard_map/all_to_all | solution.py:425
  60.2 5.0 %collective-permute-start.3 = (bf16[640,512]{1,0:T(8,128)(2,1)}, bf16[640,512]{1,0:T(8,128)(2,1)}, u32[]{:S(2)}, u32[]{:S(2)}) collective-permute-start(bf16[640,512]{1,0:T(8,128)(2,1)} %get-tuple-element.34), channel_id=1, source_target_pairs={{0,1},{1,0},{2,3},{3,2},{4,5},{5,4},{6,7},{7,6},{8,9},{9,8},{10,11... | collective-permute-start | bytes 1966088 | tf_op jit(solution)/shard_map/ppermute | solution.py:370
  65.2 7.8 %gate_up.1 = (bf16[2,160,768]{2,1,0:T(8,128)(2,1)}, bf16[2,160,768]{2,1,0:T(8,128)(2,1)}, f32[2,160,768]{2,1,0:T(8,128)}, f32[2,160,768]{2,1,0:T(8,128)}) custom-call(s32[2]{0:T(128)} %pad_add_fusion.1.where, bf16[640,512]{1,0:T(8,128)(2,1)} %get-tuple-element.31.x_ref.a_own, bf16[640,512]{1,0:T(8,128)(2,1)} %collective-permute-done.9.other_ref, ...), custom_call_target="tpu_custom_call" | custom-call | tf_op jit(solution)/shard_map/gate_up/pallas_call | solution.py:125
  73.0 3.0 %collective-permute-start.13 = (bf16[2,160,768]{2,1,0:T(8,128)(2,1)}, bf16[2,160,768]{2,1,0:T(8,128)(2,1)}, u32[]{:S(2)}, u32[]{:S(2)}) collective-permute-start(bf16[2,160,768]{2,1,0:T(8,128)(2,1)} %get-tuple-element.42), channel_id=1, source_target_pairs={{0,2},{1,3},{2,4},{3,5},{4,6},{5,7},{6,0},{7,1},{8,10},{9,11},{10,... | collective-permute-start | bytes 1474568 | tf_op jit(solution)/shard_map/ppermute | solution.py:373
  79.9 5.8 %hidden_grad.1 = (bf16[2,80,768]{2,1,0:T(8,128)(2,1)}, bf16[2,80,768]{2,1,0:T(8,128)(2,1)}, f32[2,80,768]{2,1,0:T(8,128)}, f32[2,80,768]{2,1,0:T(8,128)}) custom-call(s32[2]{0:T(128)} %pad_add_fusion.1.where, bf16[640,512]{1,0:T(8,128)(2,1)} %get-tuple-element.33.g_ref, bf16[640,512]{1,0:T(8,128)(2,1)} %collective-permute-done.3.other_ref, ...), custom_call_target="tpu_custom_call" | custom-call | tf_op jit(solution)/shard_map/hidden_grad/pallas_call | solution.py:189
  89.5 22.3 %collective-permute-done.6 = bf16[2,80,768]{2,1,0:T(8,128)(2,1)S(1)} collective-permute-done((bf16[2,80,768]{2,1,0:T(8,128)(2,1)}, bf16[2,80,768]{2,1,0:T(8,128)(2,1)S(1)}, u32[]{:S(2)}, u32[]{:S(2)}) %collective-permute-start.6) | collective-permute-done | bytes 245792 | tf_op jit(solution)/shard_map/ppermute | solution.py:373
  113.9 3.2 %collective-permute-start.7 = (bf16[80,768]{1,0:T(8,128)(2,1)S(1)}, bf16[80,768]{1,0:T(8,128)(2,1)S(1)}, u32[]{:S(2)}, u32[]{:S(2)}) collective-permute-start(bf16[80,768]{1,0:T(8,128)(2,1)S(1)} %get-tuple-element.68), channel_id=1, source_target_pairs={{0,2},{1,3},{2,4},{3,5},{4,6},{5,7},{6,0},{7,1},{8,10},{9,11},{10,... | collective-permute-start | bytes 368648 | tf_op jit(solution)/shard_map/ppermute | solution.py:373
  121.3 3.0 %collective-permute-done.7 = bf16[80,768]{1,0:T(8,128)(2,1)S(1)} collective-permute-done((bf16[80,768]{1,0:T(8,128)(2,1)S(1)}, bf16[80,768]{1,0:T(8,128)(2,1)S(1)}, u32[]{:S(2)}, u32[]{:S(2)}) %collective-permute-start.7) | collective-permute-done | bytes 122912 | tf_op jit(solution)/shard_map/ppermute | solution.py:373
  124.4 4.4 %collective-permute-done.15 = bf16[160,768]{1,0:T(8,128)(2,1)S(1)} collective-permute-done((bf16[160,768]{1,0:T(8,128)(2,1)S(1)}, bf16[160,768]{1,0:T(8,128)(2,1)S(1)}, u32[]{:S(2)}, u32[]{:S(2)}) %collective-permute-start.15) | collective-permute-done | bytes 245792 | tf_op jit(solution)/shard_map/ppermute | solution.py:376
  134.9 4.5 %collective-permute-done.21.low = bf16[160,768]{1,0:T(8,128)(2,1)S(1)} collective-permute-done((bf16[160,768]{1,0:T(8,128)(2,1)S(1)}, bf16[160,768]{1,0:T(8,128)(2,1)S(1)}, u32[]{:S(2)}, u32[]{:S(2)}) %collective-permute-start.21) | collective-permute-done | bytes 245792 | tf_op jit(solution)/shard_map/ppermute | solution.py:373
  150.2 4.9 %expert_out.1 = (bf16[32,40,512]{2,1,0:T(8,128)(2,1)}, bf16[16,40,512]{2,1,0:T(8,128)(2,1)}, bf16[640,768]{1,0:T(8,128)(2,1)}) custom-call(s32[2]{0:T(128)} %pad_add_fusion.1.where, bf16[160,768]{1,0:T(8,128)(2,1)} %copy-done.9, bf16[160,768]{1,0:T(8,128)(2,1)} %copy-done.10, bf16[160,768]{1,0:T(8,128)(2,1)} %copy-done.11, bf16[80,768]{1,0:T(8,128)(2,1)} %copy-done.16, ...), custom_call_target="tpu_custom_call" | custom-call | tf_op jit(solution)/shard_map/expert_out/pallas_call | solution.py:247
  155.1 10.5 %collective-permute-start.25 = (bf16[16,40,512]{2,1,0:T(8,128)(2,1)}, bf16[16,40,512]{2,1,0:T(8,128)(2,1)S(1)}, u32[]{:S(2)}, u32[]{:S(2)}) collective-permute-start(bf16[16,40,512]{2,1,0:T(8,128)(2,1)} %get-tuple-element.49), channel_id=1, source_target_pairs={{0,1},{1,0},{2,3},{3,2},{4,5},{5,4},{6,7},{7,6},{8,9},{9,8},{10,11... | collective-permute-start | bytes 1966088 | tf_op jit(solution)/shard_map/ppermute | solution.py:370
  171.3 3.7 %all-to-all-start.2 = ((bf16[16,80,512]{2,1,0:T(8,128)(2,1)}), bf16[16,80,512]{2,1,0:T(8,128)(2,1)S(1)}, u32[]{:S(2)}, u32[]{:S(2)}) async-start(bf16[16,80,512]{2,1,0:T(8,128)(2,1)} %bitcast.56), calls=%async_computation.2 | async-start | bytes 2621440 | tf_op jit(solution)/shard_map/all_to_all | solution.py:425
  175.0 6.3 %collective-permute-done.17.high = bf16[2,160,768]{2,1,0:T(8,128)(2,1)S(1)} collective-permute-done((bf16[2,160,768]{2,1,0:T(8,128)(2,1)S(1)}, bf16[2,160,768]{2,1,0:T(8,128)(2,1)S(1)}, u32[]{:S(2)}, u32[]{:S(2)}) %collective-permute-start.17) | collective-permute-done | bytes 491552 | tf_op jit(solution)/shard_map/ppermute | solution.py:376
  182.0 20.3 %collective-permute-done.19.far_u = bf16[160,768]{1,0:T(8,128)(2,1)S(1)} collective-permute-done((bf16[160,768]{1,0:T(8,128)(2,1)S(1)}, bf16[160,768]{1,0:T(8,128)(2,1)S(1)}, u32[]{:S(2)}, u32[]{:S(2)}) %collective-permute-start.19) | collective-permute-done | bytes 245792 | tf_op jit(solution)/shard_map/ppermute | solution.py:376
  203.0 7.7 %slot_in.1 = (bf16[32,40,512]{2,1,0:T(8,128)(2,1)}, bf16[16,40,512]{2,1,0:T(8,128)(2,1)}, bf16[2,640,768]{2,1,0:T(8,128)(2,1)}) custom-call(s32[2]{0:T(128)} %pad_add_fusion.1.where, bf16[2,160,768]{2,1,0:T(8,128)(2,1)} %copy-done.4, bf16[2,160,768]{2,1,0:T(8,128)(2,1)} %copy-done.5, bf16[2,160,768]{2,1,0:T(8,128)(2,1)} %copy-done.6, ...), custom_call_target="tpu_custom_call" | custom-call | tf_op jit(solution)/shard_map/slot_in/pallas_call | solution.py:278
  210.7 5.2 %collective-permute-start.27 = (bf16[16,40,512]{2,1,0:T(8,128)(2,1)}, bf16[16,40,512]{2,1,0:T(8,128)(2,1)S(1)}, u32[]{:S(2)}, u32[]{:S(2)}) collective-permute-start(bf16[16,40,512]{2,1,0:T(8,128)(2,1)} %get-tuple-element.53), channel_id=1, source_target_pairs={{0,1},{1,0},{2,3},{3,2},{4,5},{5,4},{6,7},{7,6},{8,9},{9,8},{10,11... | collective-permute-start | bytes 1966088 | tf_op jit(solution)/shard_map/ppermute | solution.py:370
  218.7 4.7 %all-to-all-start.3 = ((bf16[32,40,512]{2,1,0:T(8,128)(2,1)}), bf16[32,40,512]{2,1,0:T(8,128)(2,1)}, u32[]{:S(2)}, u32[]{:S(2)}) async-start(bf16[32,40,512]{2,1,0:T(8,128)(2,1)} %constant_dynamic-update-slice_fusion), calls=%async_computation.3 | async-start | bytes 2621440 | tf_op jit(solution)/shard_map/all_to_all | solution.py:421
  225.3 5.9 %weight_grad.3 = bf16[2,768,512]{2,1,0:T(8,128)(2,1)} custom-call(bf16[640,768]{1,0:T(8,128)(2,1)} %get-tuple-element.56.a_own, bf16[640,768]{1,0:T(8,128)(2,1)} %collective-permute-done.28.a_far, bf16[1,640,512]{2,1,0:T(8,128)(2,1)} %bitcast.55, bf16[1,640,512]{2,1,0:T(8,128)(2,1)} %bitcast.57), custom_call_target="tpu_custom_call" | custom-call | tf_op jit(solution)/shard_map/weight_grad/pallas_call | solution.py:315
  234.7 8.6 %weight_grad.2 = (bf16[2,512,768]{2,1,0:T(8,128)(2,1)}, bf16[2,512,768]{2,1,0:T(8,128)(2,1)}) custom-call(bf16[640,512]{1,0:T(8,128)(2,1)} %get-tuple-element.31.x_ref.a_own, bf16[640,512]{1,0:T(8,128)(2,1)} %get-tuple-element.32.a_far, bf16[2,640,768]{2,1,0:T(8,128)(2,1)} %get-tuple-element.45.b_own, bf16[2,640,768]{2,1,0:T(8,128)(2,1)} %collective-permute-done.20.b_far), custom_call_target="tpu_custom_call" | custom-call | tf_op jit(solution)/shard_map/weight_grad/pallas_call | solution.py:315
  (135 shorter events, 69.8 us)
Async XLA Ops:
  0.6 14.4 %collective-permute-start = (s32[128,8]{0,1:T(8,128)}, s32[128,8]{0,1:T(8,128)S(1)}, u32[]{:S(2)}, u32[]{:S(2)}) collective-permute-start(s32[128,8]{0,1:T(8,128)} %param.9), channel_id=1, source_target_pairs={{0,32},{32,0},{1,33},{33,1},{2,34},{34,2},{3,35},{35,3},{4,36},{36... | collective-permute-start | bytes 12296 | tf_op jit(solution)/shard_map/ppermute | solution.py:393
  6.2 27.0 %all-to-all-start = ((bf16[32,40,512]{2,1,0:T(8,128)(2,1)}), bf16[32,40,512]{2,1,0:T(8,128)(2,1)S(1)}, u32[]{:S(2)}, u32[]{:S(2)}) async-start(bf16[32,40,512]{2,1,0:T(8,128)(2,1)} %bitcast.2), calls=%async_computation | async-start | bytes 2621440 | tf_op jit(solution)/shard_map/all_to_all | solution.py:421
  13.4 15.1 %collective-permute-start.1 = (f32[128,8]{0,1:T(8,128)S(1)}, f32[128,8]{0,1:T(8,128)S(1)}, u32[]{:S(2)}, u32[]{:S(2)}) collective-permute-start(f32[128,8]{0,1:T(8,128)S(1)} %copy-done.19), channel_id=1, source_target_pairs={{0,32},{32,0},{1,33},{33,1},{2,34},{34,2},{3,35},{35,3},{4,36},{36... | collective-permute-start | bytes 12296 | tf_op jit(solution)/shard_map/ppermute | solution.py:393
  14.7 16.8 %collective-permute-start.2 = (bf16[128,512]{1,0:T(8,128)(2,1)S(1)}, bf16[128,512]{1,0:T(8,128)(2,1)S(1)}, u32[]{:S(2)}, u32[]{:S(2)}) collective-permute-start(bf16[128,512]{1,0:T(8,128)(2,1)S(1)} %copy-done.15), channel_id=1, source_target_pairs={{0,32},{32,0},{1,33},{33,1},{2,34},{34,2},{3,35},{35,3},{4,36},{36... | collective-permute-start | bytes 393224 | tf_op jit(solution)/shard_map/ppermute | solution.py:393
  34.3 23.4 %all-to-all-start.1 = ((bf16[16,80,512]{2,1,0:T(8,128)(2,1)}), bf16[16,80,512]{2,1,0:T(8,128)(2,1)}, u32[]{:S(2)}, u32[]{:S(2)}) async-start(bf16[16,80,512]{2,1,0:T(8,128)(2,1)} %bitcast.3), calls=%async_computation.1 | async-start | bytes 2621440 | tf_op jit(solution)/shard_map/all_to_all | solution.py:425
  41.0 24.2 %collective-permute-start.10 = (bf16[2,512,768]{2,1,0:T(8,128)(2,1)}, bf16[2,512,768]{2,1,0:T(8,128)(2,1)}, u32[]{:S(2)}, u32[]{:S(2)}) collective-permute-start(bf16[2,512,768]{2,1,0:T(8,128)(2,1)} %gm.3), channel_id=1, source_target_pairs={{0,1},{1,0},{2,3},{3,2},{4,5},{5,4},{6,7},{7,6},{8,9},{9,8},{10,11... | collective-permute-start | bytes 4718600 | tf_op jit(solution)/shard_map/ppermute | solution.py:370
  44.8 20.4 %collective-permute-start.11 = (bf16[2,512,768]{2,1,0:T(8,128)(2,1)}, bf16[2,512,768]{2,1,0:T(8,128)(2,1)}, u32[]{:S(2)}, u32[]{:S(2)}) collective-permute-start(bf16[2,512,768]{2,1,0:T(8,128)(2,1)} %um.3), channel_id=1, source_target_pairs={{0,1},{1,0},{2,3},{3,2},{4,5},{5,4},{6,7},{7,6},{8,9},{9,8},{10,11... | collective-permute-start | bytes 4718600 | tf_op jit(solution)/shard_map/ppermute | solution.py:370
  44.9 33.8 %collective-permute-start.4 = (bf16[2,768,512]{2,1,0:T(8,128)(2,1)S(1)}, bf16[2,768,512]{2,1,0:T(8,128)(2,1)S(1)}, u32[]{:S(2)}, u32[]{:S(2)}) collective-permute-start(bf16[2,768,512]{2,1,0:T(8,128)(2,1)S(1)} %copy-done.1), channel_id=1, source_target_pairs={{0,1},{1,0},{2,3},{3,2},{4,5},{5,4},{6,7},{7,6},{8,9},{9,8},{10,11... | collective-permute-start | bytes 4718600 | tf_op jit(solution)/shard_map/ppermute | solution.py:370
  48.5 16.8 %collective-permute-start.9 = (bf16[640,512]{1,0:T(8,128)(2,1)}, bf16[640,512]{1,0:T(8,128)(2,1)}, u32[]{:S(2)}, u32[]{:S(2)}) collective-permute-start(bf16[640,512]{1,0:T(8,128)(2,1)} %get-tuple-element.32.a_far), channel_id=1, source_target_pairs={{0,1},{1,0},{2,3},{3,2},{4,5},{5,4},{6,7},{7,6},{8,9},{9,8},{10,11... | collective-permute-start | bytes 1966088 | tf_op jit(solution)/shard_map/ppermute | solution.py:370
  60.2 18.5 %collective-permute-start.3 = (bf16[640,512]{1,0:T(8,128)(2,1)}, bf16[640,512]{1,0:T(8,128)(2,1)}, u32[]{:S(2)}, u32[]{:S(2)}) collective-permute-start(bf16[640,512]{1,0:T(8,128)(2,1)} %get-tuple-element.34), channel_id=1, source_target_pairs={{0,1},{1,0},{2,3},{3,2},{4,5},{5,4},{6,7},{7,6},{8,9},{9,8},{10,11... | collective-permute-start | bytes 1966088 | tf_op jit(solution)/shard_map/ppermute | solution.py:370
  73.0 44.6 %collective-permute-start.13 = (bf16[2,160,768]{2,1,0:T(8,128)(2,1)}, bf16[2,160,768]{2,1,0:T(8,128)(2,1)}, u32[]{:S(2)}, u32[]{:S(2)}) collective-permute-start(bf16[2,160,768]{2,1,0:T(8,128)(2,1)} %get-tuple-element.42), channel_id=1, source_target_pairs={{0,2},{1,3},{2,4},{3,5},{4,6},{5,7},{6,0},{7,1},{8,10},{9,11},{10,... | collective-permute-start | bytes 1474568 | tf_op jit(solution)/shard_map/ppermute | solution.py:373
  76.0 41.6 %collective-permute-start.12 = (bf16[2,160,768]{2,1,0:T(8,128)(2,1)}, bf16[2,160,768]{2,1,0:T(8,128)(2,1)}, u32[]{:S(2)}, u32[]{:S(2)}) collective-permute-start(bf16[2,160,768]{2,1,0:T(8,128)(2,1)} %get-tuple-element.40), channel_id=1, source_target_pairs={{0,6},{1,7},{2,0},{3,1},{4,2},{5,3},{6,4},{7,5},{8,14},{9,15},{10,... | collective-permute-start | bytes 1474568 | tf_op jit(solution)/shard_map/ppermute | solution.py:376
  85.7 26.1 %collective-permute-start.6 = (bf16[2,80,768]{2,1,0:T(8,128)(2,1)}, bf16[2,80,768]{2,1,0:T(8,128)(2,1)S(1)}, u32[]{:S(2)}, u32[]{:S(2)}) collective-permute-start(bf16[2,80,768]{2,1,0:T(8,128)(2,1)} %get-tuple-element.38), channel_id=1, source_target_pairs={{0,2},{1,3},{2,4},{3,5},{4,6},{5,7},{6,0},{7,1},{8,10},{9,11},{10,... | collective-permute-start | bytes 737288 | tf_op jit(solution)/shard_map/ppermute | solution.py:373
  87.0 25.7 %collective-permute-start.5 = (bf16[2,80,768]{2,1,0:T(8,128)(2,1)}, bf16[2,80,768]{2,1,0:T(8,128)(2,1)S(1)}, u32[]{:S(2)}, u32[]{:S(2)}) collective-permute-start(bf16[2,80,768]{2,1,0:T(8,128)(2,1)} %get-tuple-element.36), channel_id=1, source_target_pairs={{0,6},{1,7},{2,0},{3,1},{4,2},{5,3},{6,4},{7,5},{8,14},{9,15},{10,... | collective-permute-start | bytes 737288 | tf_op jit(solution)/shard_map/ppermute | solution.py:376
  113.9 10.4 %collective-permute-start.7 = (bf16[80,768]{1,0:T(8,128)(2,1)S(1)}, bf16[80,768]{1,0:T(8,128)(2,1)S(1)}, u32[]{:S(2)}, u32[]{:S(2)}) collective-permute-start(bf16[80,768]{1,0:T(8,128)(2,1)S(1)} %get-tuple-element.68), channel_id=1, source_target_pairs={{0,2},{1,3},{2,4},{3,5},{4,6},{5,7},{6,0},{7,1},{8,10},{9,11},{10,... | collective-permute-start | bytes 368648 | tf_op jit(solution)/shard_map/ppermute | solution.py:373
  143.3 23.4 %collective-permute-start.16 = (bf16[2,160,768]{2,1,0:T(8,128)(2,1)S(1)}, bf16[2,160,768]{2,1,0:T(8,128)(2,1)S(1)}, u32[]{:S(2)}, u32[]{:S(2)}) collective-permute-start(bf16[2,160,768]{2,1,0:T(8,128)(2,1)S(1)} %pad_maximum_fusion.1.own), channel_id=1, source_target_pairs={{0,2},{1,3},{2,4},{3,5},{4,6},{5,7},{6,0},{7,1},{8,10},{9,11},{10,... | collective-permute-start | bytes 1474568 | tf_op jit(solution)/shard_map/ppermute | solution.py:373
  155.1 15.3 %collective-permute-start.25 = (bf16[16,40,512]{2,1,0:T(8,128)(2,1)}, bf16[16,40,512]{2,1,0:T(8,128)(2,1)S(1)}, u32[]{:S(2)}, u32[]{:S(2)}) collective-permute-start(bf16[16,40,512]{2,1,0:T(8,128)(2,1)} %get-tuple-element.49), channel_id=1, source_target_pairs={{0,1},{1,0},{2,3},{3,2},{4,5},{5,4},{6,7},{7,6},{8,9},{9,8},{10,11... | collective-permute-start | bytes 1966088 | tf_op jit(solution)/shard_map/ppermute | solution.py:370
  165.6 15.6 %collective-permute-start.17 = (bf16[2,160,768]{2,1,0:T(8,128)(2,1)S(1)}, bf16[2,160,768]{2,1,0:T(8,128)(2,1)S(1)}, u32[]{:S(2)}, u32[]{:S(2)}) collective-permute-start(bf16[2,160,768]{2,1,0:T(8,128)(2,1)S(1)} %pad_maximum_fusion.1.own), channel_id=1, source_target_pairs={{0,6},{1,7},{2,0},{3,1},{4,2},{5,3},{6,4},{7,5},{8,14},{9,15},{10,... | collective-permute-start | bytes 1474568 | tf_op jit(solution)/shard_map/ppermute | solution.py:376
  167.5 14.5 %collective-permute-start.18 = (bf16[160,768]{1,0:T(8,128)(2,1)}, bf16[160,768]{1,0:T(8,128)(2,1)S(1)}, u32[]{:S(2)}, u32[]{:S(2)}) collective-permute-start(bf16[160,768]{1,0:T(8,128)(2,1)} %slice_bitcast_fusion.1), channel_id=1, source_target_pairs={{0,2},{1,3},{2,4},{3,5},{4,6},{5,7},{6,0},{7,1},{8,10},{9,11},{10,... | collective-permute-start | bytes 737288 | tf_op jit(solution)/shard_map/ppermute | solution.py:373
  171.3 47.5 %all-to-all-start.2 = ((bf16[16,80,512]{2,1,0:T(8,128)(2,1)}), bf16[16,80,512]{2,1,0:T(8,128)(2,1)S(1)}, u32[]{:S(2)}, u32[]{:S(2)}) async-start(bf16[16,80,512]{2,1,0:T(8,128)(2,1)} %bitcast.56), calls=%async_computation.2 | async-start | bytes 2621440 | tf_op jit(solution)/shard_map/all_to_all | solution.py:425
  181.3 21.0 %collective-permute-start.19 = (bf16[160,768]{1,0:T(8,128)(2,1)S(1)}, bf16[160,768]{1,0:T(8,128)(2,1)S(1)}, u32[]{:S(2)}, u32[]{:S(2)}) collective-permute-start(bf16[160,768]{1,0:T(8,128)(2,1)S(1)} %slice_bitcast_fusion), channel_id=1, source_target_pairs={{0,6},{1,7},{2,0},{3,1},{4,2},{5,3},{6,4},{7,5},{8,14},{9,15},{10,... | collective-permute-start | bytes 737288 | tf_op jit(solution)/shard_map/ppermute | solution.py:376
  218.7 26.8 %all-to-all-start.3 = ((bf16[32,40,512]{2,1,0:T(8,128)(2,1)}), bf16[32,40,512]{2,1,0:T(8,128)(2,1)}, u32[]{:S(2)}, u32[]{:S(2)}) async-start(bf16[32,40,512]{2,1,0:T(8,128)(2,1)} %constant_dynamic-update-slice_fusion), calls=%async_computation.3 | async-start | bytes 2621440 | tf_op jit(solution)/shard_map/all_to_all | solution.py:421
  223.4 11.3 %collective-permute-start.20 = (bf16[2,640,768]{2,1,0:T(8,128)(2,1)}, bf16[2,640,768]{2,1,0:T(8,128)(2,1)}, u32[]{:S(2)}, u32[]{:S(2)}) collective-permute-start(bf16[2,640,768]{2,1,0:T(8,128)(2,1)} %get-tuple-element.45.b_own), channel_id=1, source_target_pairs={{0,1},{1,0},{2,3},{3,2},{4,5},{5,4},{6,7},{7,6},{8,9},{9,8},{10,11... | collective-permute-start | bytes 5898248 | tf_op jit(solution)/shard_map/ppermute | solution.py:370
  232.2 12.6 %collective-permute-start.26 = (f32[128,512]{1,0:T(8,128)S(1)}, f32[128,512]{1,0:T(8,128)S(1)}, u32[]{:S(2)}, u32[]{:S(2)}) collective-permute-start(f32[128,512]{1,0:T(8,128)S(1)} %convolution_add_fusion.2), channel_id=1, source_target_pairs={{0,32},{32,0},{1,33},{33,1},{2,34},{34,2},{3,35},{35,3},{4,36},{36... | collective-permute-start | bytes 786440 | tf_op jit(solution)/shard_map/ppermute | solution.py:393
  (29 other events, 275.9 us)
